TPU v7x, 512 devices: a whole 4x8x8 slice. The times are simulated.
512 devices in a mesh: ctx: 16 (over z, core), head: 32 (over x, y).
Axes of the slice: x: 4, y: 8, z: 8, core: 2. Of those that a mesh axis runs over, the one named last changes fastest.
Arguments:
- x_in: bfloat16 [4096, 16384], P(('ctx', 'head')), may hold values from -6 to 6
- grad_y: bfloat16 [4096, 16384], P(('ctx', 'head')), may hold values from -6 to 6
- b_in: bfloat16 [4096, 2048], P(('ctx', 'head')), may hold values from -0.29882812 to 0.29882812
- c_in: bfloat16 [4096, 2048], P(('ctx', 'head')), may hold values from -0.375 to 0.375
- dt: bfloat16 [4096, 256], P(('ctx', 'head')), may hold values from 0.25 to 2
- conv_weight: float32 [4, 16384], P(None, 'head'), may hold values from -3 to 3
- conv_bias: float32 [16384], P('head'), may hold values from -3 to 3
- decay_rate: float32 [256], P('head'), may hold values from 1e-05 to 0.02
- skip: float32 [256], P('head'), may hold values from 0.5 to 1.5
Outputs:
- grad_x: bfloat16 [4096, 16384], P(('ctx', 'head'))
- grad_b: bfloat16 [4096, 2048], P(('ctx', 'head'))
- grad_c: bfloat16 [4096, 2048], P(('ctx', 'head'))
- grad_dt: float32 [4096, 256], P(('ctx', 'head'))
All inputs are finite; a program needn't handle non-finite values.
Results may differ from a plain program's by a relative error of at most 0.001.
Values may be sent and summed in bfloat16 or wider, within the bound.
A program may use at most 64 MiB of HBM per device.

v0:
```python
import math

import jax
import jax.numpy as jnp
from jax import lax
from jax.sharding import PartitionSpec as P

HEAD_DIM = 64
STATE = 256
GROUPS = 8
CONV = 4


HIGH = lax.Precision.HIGHEST


def passed_along(value, axis, by):
    count = lax.axis_size(axis)
    pairs = [(i, i + by) for i in range(count) if 0 <= i + by < count]
    return lax.ppermute(value, axis, pairs)


def entering(value, axis, combine, identity, reverse):
    count, place = (lax.axis_size(axis), lax.axis_index(axis))
    everything = jax.tree.map(lambda part: lax.all_gather(part, axis), value)
    start = jax.tree.map(
        lambda part, zero: jnp.broadcast_to(jnp.asarray(zero, part.dtype), part.shape),
        value,
        identity,
    )

    def hop(k, before):
        at = count - 1 - k if reverse else k
        reached = at > place if reverse else at < place
        new = combine(before, jax.tree.map(lambda part: part[at], everything))
        return jax.tree.map(lambda a, b: jnp.where(reached, a, b), new, before)

    return lax.fori_loop(0, count, hop, start)


def conv_silu(padded, weight, bias):
    length = padded.shape[0] - CONV + 1
    summed = bias[None, :] + weight[0][None, :] * padded[0:length]
    for k in range(1, CONV):
        summed = summed + weight[k][None, :] * padded[k : k + length]
    return jax.nn.silu(summed)


def head_forward(
    ext_rows, dt_head, gram_blocks, b_rows, c_rows, weight, bias, head_rate, skip_head, state_in
):
    activ = conv_silu(ext_rows, weight, bias)
    length = activ.shape[0]
    width = gram_blocks.shape[1]
    count = length // width
    causal = lax.broadcasted_iota(jnp.int32, (width, width), 0) >= lax.broadcasted_iota(
        jnp.int32, (width, width), 1
    )
    pieces = (
        activ.reshape(count, width, HEAD_DIM),
        dt_head.reshape(count, width),
        gram_blocks,
        b_rows.reshape(count, width, STATE),
        c_rows.reshape(count, width, STATE),
    )

    def advance(carried, piece):
        act_part, dt_part, gram_part, b_part, c_part = piece
        cumul = jnp.cumsum(-dt_part * head_rate)
        gaps = cumul[:, None] - cumul[None, :]
        decay_mat = jnp.where(causal, jnp.exp(jnp.where(causal, gaps, 0.0)), 0.0)
        mixing = decay_mat * gram_part * dt_part[None, :]
        output = jnp.dot(mixing, act_part, precision=HIGH)
        output = output + jnp.exp(cumul)[:, None] * jnp.dot(c_part, carried.T, precision=HIGH)
        tail_wt = jnp.exp(cumul[-1] - cumul) * dt_part
        carried = jnp.exp(cumul[-1]) * carried + jnp.dot(
            (act_part * tail_wt[:, None]).T, b_part, precision=HIGH
        )
        return (carried, output)

    state_out, outputs = lax.scan(advance, state_in, pieces)
    output = outputs.reshape(length, HEAD_DIM) + skip_head * activ
    return (output, state_out)


def forward_combine(earlier, later):
    return (earlier[0] * later[0], later[0][:, None, None] * earlier[1] + later[1])


def backward_combine(earlier, later):
    return (earlier[0] * later[0], later[1] + later[0][:, None, None] * earlier[1])


def shards(x_in, grad_y, b_in, c_in, dt, conv_weight, conv_bias, decay_rate, skip):
    n_head = lax.axis_size("head")
    per_group = n_head // GROUPS
    tok_dev = x_in.shape[0]
    heads_dev = decay_rate.shape[0]
    x_rows, dy_rows, dt_rows = (
        lax.all_to_all(x_in, "head", split_axis=1, concat_axis=0, tiled=True),
        lax.all_to_all(grad_y, "head", split_axis=1, concat_axis=0, tiled=True),
        lax.all_to_all(dt, "head", split_axis=1, concat_axis=0, tiled=True),
    )
    b_all, c_all = (
        lax.all_gather(b_in, "head", axis=0, tiled=True),
        lax.all_gather(c_in, "head", axis=0, tiled=True),
    )
    first = lax.axis_index("head") // per_group * STATE
    b_rows = lax.dynamic_slice_in_dim(b_all, first, STATE, 1)
    c_rows = lax.dynamic_slice_in_dim(c_all, first, STATE, 1)
    length = x_rows.shape[0]
    width = math.gcd(length, 128)
    count = length // width
    edge = passed_along(x_rows[length - CONV + 1 :], "ctx", 1)
    ext_rows = jnp.concatenate([edge, x_rows], axis=0).astype(jnp.float32)
    b_mat = b_rows.astype(jnp.float32)
    c_mat = c_rows.astype(jnp.float32)
    dt_mat = dt_rows.astype(jnp.float32)
    dy_mat = dy_rows.astype(jnp.float32).reshape(length, heads_dev, HEAD_DIM)
    activ = conv_silu(ext_rows, conv_weight, conv_bias).reshape(length, heads_dev, HEAD_DIM)
    cumul = jnp.cumsum(-dt_mat * decay_rate[None, :], axis=0)
    block_decay = jnp.exp(cumul[-1])
    tail_wt = jnp.exp(cumul[-1][None, :] - cumul) * dt_mat
    local_state = jnp.einsum("shp,sn->hpn", activ * tail_wt[:, :, None], b_mat, precision=HIGH)
    local_pull = jnp.einsum(
        "shp,sn->hpn", dy_mat * jnp.exp(cumul)[:, :, None], c_mat, precision=HIGH
    )
    identity = (
        jnp.ones((heads_dev,), jnp.float32),
        jnp.zeros((heads_dev, HEAD_DIM, STATE), jnp.float32),
    )
    _, state_in = entering((block_decay, local_state), "ctx", forward_combine, identity, False)
    _, state_grad = entering((block_decay, local_pull), "ctx", backward_combine, identity, True)
    b_blocks = b_mat.reshape(count, width, STATE)
    c_blocks = c_mat.reshape(count, width, STATE)
    gram_blocks = jnp.einsum("cwn,cvn->cwv", c_blocks, b_blocks, precision=HIGH)

    def head_step(sums, pieces):
        ext_head, dt_head, weight, bias, head_rate, skip_head, head_state, dy_head, head_grad = (
            pieces
        )

        def forward_fn(ext_arg, dt_arg, gram_arg, b_arg, c_arg):
            return head_forward(
                ext_arg,
                dt_arg,
                gram_arg,
                b_arg,
                c_arg,
                weight,
                bias,
                head_rate,
                skip_head,
                head_state,
            )

        _, pullback = jax.vjp(forward_fn, ext_head, dt_head, gram_blocks, b_mat, c_mat)
        g_ext, g_dt, g_gram, g_b, g_c = pullback((dy_head, head_grad))
        return ((sums[0] + g_gram, sums[1] + g_b, sums[2] + g_c), (g_ext, g_dt))

    ext_heads = ext_rows.reshape(length + CONV - 1, heads_dev, HEAD_DIM).transpose(1, 0, 2)
    weight_heads = conv_weight.reshape(CONV, heads_dev, HEAD_DIM).transpose(1, 0, 2)
    bias_heads = conv_bias.reshape(heads_dev, HEAD_DIM)
    start = (
        jnp.zeros((count, width, width), jnp.float32),
        jnp.zeros((length, STATE), jnp.float32),
        jnp.zeros((length, STATE), jnp.float32),
    )
    inputs = (
        ext_heads,
        dt_mat.T,
        weight_heads,
        bias_heads,
        decay_rate,
        skip,
        state_in,
        dy_mat.transpose(1, 0, 2),
        state_grad,
    )
    sums, per_head = lax.scan(head_step, start, inputs)
    g_gram, g_b, g_c = sums
    g_b = g_b + jnp.einsum("cwv,cwn->cvn", g_gram, c_blocks, precision=HIGH).reshape(length, STATE)
    g_c = g_c + jnp.einsum("cwv,cvn->cwn", g_gram, b_blocks, precision=HIGH).reshape(length, STATE)
    g_ext = per_head[0].transpose(1, 0, 2).reshape(length + CONV - 1, heads_dev * HEAD_DIM)
    g_dt = per_head[1].T
    carried_back = passed_along(g_ext[: CONV - 1], "ctx", -1)
    g_local = g_ext[CONV - 1 :]
    g_local = g_local.at[length - CONV + 1 :].add(carried_back)
    grad_x = lax.all_to_all(
        g_local.astype(jnp.bfloat16), "head", split_axis=0, concat_axis=1, tiled=True
    )
    grad_dt, b_parts, c_parts = (
        lax.all_to_all(g_dt, "head", split_axis=0, concat_axis=1, tiled=True),
        lax.all_to_all(g_b, "head", split_axis=0, concat_axis=1, tiled=True),
        lax.all_to_all(g_c, "head", split_axis=0, concat_axis=1, tiled=True),
    )
    grad_b = (
        b_parts.reshape(tok_dev, GROUPS, per_group, STATE)
        .sum(axis=2)
        .reshape(tok_dev, GROUPS * STATE)
    )
    grad_c = (
        c_parts.reshape(tok_dev, GROUPS, per_group, STATE)
        .sum(axis=2)
        .reshape(tok_dev, GROUPS * STATE)
    )
    return (grad_x, grad_b.astype(jnp.bfloat16), grad_c.astype(jnp.bfloat16), grad_dt)


def solution(mesh):
    in_specs = (
        P(("ctx", "head"), None),
        P(("ctx", "head"), None),
        P(("ctx", "head"), None),
        P(("ctx", "head"), None),
        P(("ctx", "head"), None),
        P(None, "head"),
        P("head"),
        P("head"),
        P("head"),
    )
    out_specs = (
        P(("ctx", "head"), None),
        P(("ctx", "head"), None),
        P(("ctx", "head"), None),
        P(("ctx", "head"), None),
    )
    return jax.shard_map(shards, mesh=mesh, in_specs=in_specs, out_specs=out_specs, check_vma=False)
```

profile of v0, /device:TPU:1, one launch (start us, length us, event | category | flops | bytes accessed | tf_op | source)
XLA Modules:
  0.0 932.1 jit_solution(3826005962519937768)
XLA Ops:
  45.9 48.0 %all-gather.8.cloned.1.call-done = bf16[256,2048]{1,0:T(8,128)(2,1)} async-done(((bf16[8,2048]{1,0:T(8,128)(2,1)}), bf16[256,2048]{1,0:T(8,128)(2,1)}) %all-gather.8.cloned.1.call-update) | async-done | bytes 1048592 | tf_op jit(solution)/shard_map/all_gather | solution.py:106
  123.4 53.1 %all-gather.10.cloned.1.call-done = bf16[256,2048]{1,0:T(8,128)(2,1)} async-done(((bf16[8,2048]{1,0:T(8,128)(2,1)}), bf16[256,2048]{1,0:T(8,128)(2,1)}) %all-gather.10.cloned.1.call-update) | async-done | bytes 1048592 | tf_op jit(solution)/shard_map/all_gather | solution.py:105
  180.1 22.8 %all-gather.2 = f32[16,1,8]{2,1,0:T(1,128)S(1)} all-gather(f32[1,1,8]{2,1,0:T(1,128)S(1)} %bitcast.532), channel_id=1, replica_groups=mesh['ctx'=16,'head'=32] {'ctx'}, dimensions={0}, use_global_device_ids=true | all-gather | bytes 544 | tf_op jit(solution)/shard_map/all_gather | solution.py:25
  204.4 36.4 %all-gather.12.cloned.1.call-done = f32[128,64,256]{2,1,0:T(8,128)} async-done(((f32[8,64,256]{2,1,0:T(8,128)}), f32[128,64,256]{2,1,0:T(8,128)}) %all-gather.12.cloned.1.call-update) | async-done | bytes 8388624 | tf_op jit(solution)/shard_map/all_gather | solution.py:25
  240.8 34.0 %while.180 = (s32[]{:T(128)}, f32[8,64,256]{2,1,0:T(8,128)}, s32[]{:T(128)}, f32[16,8,64,256]{3,2,1,0:T(8,128)}, f32[16,8]{1,0:T(8,128)S(1)}, /*index=5*/s32[]{:T(128)}, s32[]{:T(128)}, s32[]{:T(128)}, s32[]{:T(128)}) while((s32[]{:T(128)}, f32[8,64,256]{2,1,0:T(8,128)}, s32[]{:T(128)}, f32[16,8,64,256]{3,2,1,0:T(8,128)}, ...), condition=%wide.region_5.6_spmd.clone, body=%wide.region_4.5_spmd.clone.sunk | while | flops 524296 | bytes 1573127 | solution.py:38
  274.8 25.4 %all-gather.14.cloned.1.call-done = f32[128,64,256]{2,1,0:T(8,128)} async-done(((f32[8,64,256]{2,1,0:T(8,128)}), f32[128,64,256]{2,1,0:T(8,128)}) %all-gather.14.cloned.1.call-update) | async-done | bytes 8388624 | tf_op jit(solution)/shard_map/all_gather | solution.py:25
  300.2 19.4 %while.181 = (s32[]{:T(128)}, f32[8,64,256]{2,1,0:T(8,128)S(1)}, s32[]{:T(128)}, f32[16,8]{1,0:T(8,128)S(1)}, f32[16,8,64,256]{3,2,1,0:T(8,128)}, /*index=5*/s32[]{:T(128)}, s32[]{:T(128)}) while((s32[]{:T(128)}, f32[8,64,256]{2,1,0:T(8,128)S(1)}, s32[]{:T(128)}, f32[16,8]{1,0:T(8,128)S(1)}, f32[16,8,64,256]{3,2,1,0:T(8,128)}, ...), condition=%wide.region_3.4_spmd.clone, body=%wide.region_2.3_spmd.clone.sunk | while | flops 524292 | bytes 1573065 | solution.py:38
  319.6 532.5 %while.184 = (s32[]{:T(128)}, f32[2,128,128]{2,1,0:T(8,128)}, f32[256,256]{1,0:T(8,128)}, f32[256,256]{1,0:T(8,128)}, f32[8,259,64]{1,2,0:T(8,128)}, /*index=5*/...) while((s32[]{:T(128)}, f32[2,128,128]{2,1,0:T(8,128)}, ...), condition=%wide.region_20.21_spmd.clone, body=%wide.region_6.20_spmd.clone.sunk | while | flops 177621440 | bytes 10403926 | solution.py:180
  327.2 12.2 %while.185 = (s32[]{:T(128)}, f32[64,256]{1,0:T(8,128)S(1)}, f32[2,128,128]{2,1,0:T(8,128)S(1)}, f32[2,128,128]{2,1,0:T(8,128)S(1)}, f32[2,1,128]{2,1,0:T(1,128)...) while((s32[]{:T(128)}, f32[64,256]{1,0:T(8,128)S(1)}, ...), condition=%wide.region_9.9_spmd.clone.clone, body=%wide.region_7.8_spmd.clone.clone.sunk | while | flops 50496128 | bytes 1198381 | solution.py:81
  343.5 32.7 %while.186 = (s32[]{:T(128)}, f32[64,256]{1,0:T(8,128)S(1)}, f32[2,128,64]{1,2,0:T(8,128)}, f32[2,128]{1,0:T(2,128)}, f32[2,128,128]{2,1,0:T(8,128)}, /*index=5*...) while((s32[]{:T(128)}, f32[64,256]{1,0:T(8,128)S(1)}, ...), condition=%wide.region_19.19_spmd.clone.clone, body=%wide.region_10.18_spmd.clone.clone.sunk | while | flops 126174464 | bytes 2319733 | solution.py:81
  392.8 12.2 %while.185 = (s32[]{:T(128)}, f32[64,256]{1,0:T(8,128)S(1)}, f32[2,128,128]{2,1,0:T(8,128)S(1)}, f32[2,128,128]{2,1,0:T(8,128)S(1)}, f32[2,1,128]{2,1,0:T(1,128)...) while((s32[]{:T(128)}, f32[64,256]{1,0:T(8,128)S(1)}, ...), condition=%wide.region_9.9_spmd.clone.clone, body=%wide.region_7.8_spmd.clone.clone.sunk | while | flops 50496128 | bytes 1198381 | solution.py:81
  409.1 32.7 %while.186 = (s32[]{:T(128)}, f32[64,256]{1,0:T(8,128)S(1)}, f32[2,128,64]{1,2,0:T(8,128)}, f32[2,128]{1,0:T(2,128)}, f32[2,128,128]{2,1,0:T(8,128)}, /*index=5*...) while((s32[]{:T(128)}, f32[64,256]{1,0:T(8,128)S(1)}, ...), condition=%wide.region_19.19_spmd.clone.clone, body=%wide.region_10.18_spmd.clone.clone.sunk | while | flops 126174464 | bytes 2319733 | solution.py:81
  459.5 12.2 %while.185 = (s32[]{:T(128)}, f32[64,256]{1,0:T(8,128)S(1)}, f32[2,128,128]{2,1,0:T(8,128)S(1)}, f32[2,128,128]{2,1,0:T(8,128)S(1)}, f32[2,1,128]{2,1,0:T(1,128)...) while((s32[]{:T(128)}, f32[64,256]{1,0:T(8,128)S(1)}, ...), condition=%wide.region_9.9_spmd.clone.clone, body=%wide.region_7.8_spmd.clone.clone.sunk | while | flops 50496128 | bytes 1198381 | solution.py:81
  475.8 32.7 %while.186 = (s32[]{:T(128)}, f32[64,256]{1,0:T(8,128)S(1)}, f32[2,128,64]{1,2,0:T(8,128)}, f32[2,128]{1,0:T(2,128)}, f32[2,128,128]{2,1,0:T(8,128)}, /*index=5*...) while((s32[]{:T(128)}, f32[64,256]{1,0:T(8,128)S(1)}, ...), condition=%wide.region_19.19_spmd.clone.clone, body=%wide.region_10.18_spmd.clone.clone.sunk | while | flops 126174464 | bytes 2319733 | solution.py:81
  526.2 12.2 %while.185 = (s32[]{:T(128)}, f32[64,256]{1,0:T(8,128)S(1)}, f32[2,128,128]{2,1,0:T(8,128)S(1)}, f32[2,128,128]{2,1,0:T(8,128)S(1)}, f32[2,1,128]{2,1,0:T(1,128)...) while((s32[]{:T(128)}, f32[64,256]{1,0:T(8,128)S(1)}, ...), condition=%wide.region_9.9_spmd.clone.clone, body=%wide.region_7.8_spmd.clone.clone.sunk | while | flops 50496128 | bytes 1198381 | solution.py:81
  542.5 32.7 %while.186 = (s32[]{:T(128)}, f32[64,256]{1,0:T(8,128)S(1)}, f32[2,128,64]{1,2,0:T(8,128)}, f32[2,128]{1,0:T(2,128)}, f32[2,128,128]{2,1,0:T(8,128)}, /*index=5*...) while((s32[]{:T(128)}, f32[64,256]{1,0:T(8,128)S(1)}, ...), condition=%wide.region_19.19_spmd.clone.clone, body=%wide.region_10.18_spmd.clone.clone.sunk | while | flops 126174464 | bytes 2319733 | solution.py:81
  592.9 12.2 %while.185 = (s32[]{:T(128)}, f32[64,256]{1,0:T(8,128)S(1)}, f32[2,128,128]{2,1,0:T(8,128)S(1)}, f32[2,128,128]{2,1,0:T(8,128)S(1)}, f32[2,1,128]{2,1,0:T(1,128)...) while((s32[]{:T(128)}, f32[64,256]{1,0:T(8,128)S(1)}, ...), condition=%wide.region_9.9_spmd.clone.clone, body=%wide.region_7.8_spmd.clone.clone.sunk | while | flops 50496128 | bytes 1198381 | solution.py:81
  609.2 32.7 %while.186 = (s32[]{:T(128)}, f32[64,256]{1,0:T(8,128)S(1)}, f32[2,128,64]{1,2,0:T(8,128)}, f32[2,128]{1,0:T(2,128)}, f32[2,128,128]{2,1,0:T(8,128)}, /*index=5*...) while((s32[]{:T(128)}, f32[64,256]{1,0:T(8,128)S(1)}, ...), condition=%wide.region_19.19_spmd.clone.clone, body=%wide.region_10.18_spmd.clone.clone.sunk | while | flops 126174464 | bytes 2319733 | solution.py:81
  659.5 12.2 %while.185 = (s32[]{:T(128)}, f32[64,256]{1,0:T(8,128)S(1)}, f32[2,128,128]{2,1,0:T(8,128)S(1)}, f32[2,128,128]{2,1,0:T(8,128)S(1)}, f32[2,1,128]{2,1,0:T(1,128)...) while((s32[]{:T(128)}, f32[64,256]{1,0:T(8,128)S(1)}, ...), condition=%wide.region_9.9_spmd.clone.clone, body=%wide.region_7.8_spmd.clone.clone.sunk | while | flops 50496128 | bytes 1198381 | solution.py:81
  675.9 32.7 %while.186 = (s32[]{:T(128)}, f32[64,256]{1,0:T(8,128)S(1)}, f32[2,128,64]{1,2,0:T(8,128)}, f32[2,128]{1,0:T(2,128)}, f32[2,128,128]{2,1,0:T(8,128)}, /*index=5*...) while((s32[]{:T(128)}, f32[64,256]{1,0:T(8,128)S(1)}, ...), condition=%wide.region_19.19_spmd.clone.clone, body=%wide.region_10.18_spmd.clone.clone.sunk | while | flops 126174464 | bytes 2319733 | solution.py:81
  726.2 12.2 %while.185 = (s32[]{:T(128)}, f32[64,256]{1,0:T(8,128)S(1)}, f32[2,128,128]{2,1,0:T(8,128)S(1)}, f32[2,128,128]{2,1,0:T(8,128)S(1)}, f32[2,1,128]{2,1,0:T(1,128)...) while((s32[]{:T(128)}, f32[64,256]{1,0:T(8,128)S(1)}, ...), condition=%wide.region_9.9_spmd.clone.clone, body=%wide.region_7.8_spmd.clone.clone.sunk | while | flops 50496128 | bytes 1198381 | solution.py:81
  742.6 32.7 %while.186 = (s32[]{:T(128)}, f32[64,256]{1,0:T(8,128)S(1)}, f32[2,128,64]{1,2,0:T(8,128)}, f32[2,128]{1,0:T(2,128)}, f32[2,128,128]{2,1,0:T(8,128)}, /*index=5*...) while((s32[]{:T(128)}, f32[64,256]{1,0:T(8,128)S(1)}, ...), condition=%wide.region_19.19_spmd.clone.clone, body=%wide.region_10.18_spmd.clone.clone.sunk | while | flops 126174464 | bytes 2319733 | solution.py:81
  792.9 12.2 %while.185 = (s32[]{:T(128)}, f32[64,256]{1,0:T(8,128)S(1)}, f32[2,128,128]{2,1,0:T(8,128)S(1)}, f32[2,128,128]{2,1,0:T(8,128)S(1)}, f32[2,1,128]{2,1,0:T(1,128)...) while((s32[]{:T(128)}, f32[64,256]{1,0:T(8,128)S(1)}, ...), condition=%wide.region_9.9_spmd.clone.clone, body=%wide.region_7.8_spmd.clone.clone.sunk | while | flops 50496128 | bytes 1198381 | solution.py:81
  809.3 32.7 %while.186 = (s32[]{:T(128)}, f32[64,256]{1,0:T(8,128)S(1)}, f32[2,128,64]{1,2,0:T(8,128)}, f32[2,128]{1,0:T(2,128)}, f32[2,128,128]{2,1,0:T(8,128)}, /*index=5*...) while((s32[]{:T(128)}, f32[64,256]{1,0:T(8,128)S(1)}, ...), condition=%wide.region_19.19_spmd.clone.clone, body=%wide.region_10.18_spmd.clone.clone.sunk | while | flops 126174464 | bytes 2319733 | solution.py:81
  (1247 shorter events, 698.9 us)
Async XLA Ops:
  7.2 95.2 %copy-start.11 = (f32[4,512]{1,0:T(4,128)S(1)}, f32[4,512]{1,0:T(4,128)}, u32[]{:S(2)}) copy-start(f32[4,512]{1,0:T(4,128)} %param.26) | copy-start | bytes 24580
  7.2 115.6 %copy-start.12 = (f32[512]{0:T(512)S(1)}, f32[512]{0:T(512)}, u32[]{:S(2)}) copy-start(f32[512]{0:T(512)} %param.27) | copy-start | bytes 6148
  7.2 86.7 %all-gather.8.cloned.1.call-start = ((), (), s32[]{:S(2)}) async-start(), calls=%async_computation.7 | async-start | bytes 1081344 | tf_op jit(solution)/shard_map/all_gather | solution.py:106
  7.9 168.6 %all-gather.10.cloned.1.call-start = ((), (), s32[]{:S(2)}) async-start(), calls=%async_computation.8 | async-start | bytes 1081344 | tf_op jit(solution)/shard_map/all_gather | solution.py:105
  10.1 19.4 %all-to-all-start.1 = ((bf16[8,32,8]{2,0,1:T(8,128)(2,1)}), bf16[8,32,8]{2,0,1:T(8,128)(2,1)S(1)}, u32[]{:S(2)}, u32[]{:S(2)}) async-start(bf16[8,32,8]{2,0,1:T(8,128)(2,1)} %copy.117), calls=%async_computation.1 | async-start | bytes 131072 | tf_op jit(solution)/shard_map/all_to_all | solution.py:102
  29.5 13.5 %all-to-all-start = ((bf16[8,32,512]{2,0,1:T(8,128)(2,1)}), bf16[8,32,512]{2,0,1:T(8,128)(2,1)S(1)}, u32[]{:S(2)}, u32[]{:S(2)}) async-start(bf16[8,32,512]{2,0,1:T(8,128)(2,1)} %bitcast.520), calls=%async_computation | async-start | bytes 524288 | tf_op jit(solution)/shard_map/all_to_all | solution.py:101
  33.4 207.4 %all-gather.12.cloned.1.call-start = ((), (), s32[]{:S(2)}) async-start(), calls=%async_computation.9 | async-start | bytes 8912896 | tf_op jit(solution)/shard_map/all_gather | solution.py:25
  94.8 146.0 %copy-start.2 = (bf16[256,256]{1,0:T(8,128)(2,1)}, bf16[256,256]{1,0:T(8,128)(2,1)S(1)}, u32[]{:S(2)}) copy-start(bf16[256,256]{1,0:T(8,128)(2,1)S(1)} %get-tuple-element.2368) | copy-start | bytes 393220
  96.7 15.4 %all-to-all-start.2 = ((bf16[8,32,512]{2,0,1:T(8,128)(2,1)}), bf16[8,32,512]{2,0,1:T(8,128)(2,1)S(1)}, u32[]{:S(2)}, u32[]{:S(2)}) async-start(bf16[8,32,512]{2,0,1:T(8,128)(2,1)} %bitcast.16), calls=%async_computation.2 | async-start | bytes 524288 | tf_op jit(solution)/shard_map/all_to_all | solution.py:100
  102.4 197.9 %all-gather.14.cloned.1.call-start = ((), (), s32[]{:S(2)}) async-start(), calls=%async_computation.10 | async-start | bytes 8912896 | tf_op jit(solution)/shard_map/all_gather | solution.py:25
  112.0 10.7 %collective-permute-start = (bf16[3,512]{1,0:T(4,128)(2,1)S(1)}, bf16[3,512]{1,0:T(4,128)(2,1)S(1)}, u32[]{:S(2)}, u32[]{:S(2)}) collective-permute-start(bf16[3,512]{1,0:T(4,128)(2,1)S(1)} %slice.212), channel_id=1, source_target_pairs={{0,32},{32,64},{64,96},{96,128},{128,160},{160,192},{192,224},{224... | collective-permute-start | bytes 9224 | tf_op jit(solution)/shard_map/ppermute | solution.py:20
  177.4 122.8 %copy-start.1 = (bf16[256,256]{1,0:T(8,128)(2,1)}, bf16[256,256]{1,0:T(8,128)(2,1)S(1)}, u32[]{:S(2)}) copy-start(bf16[256,256]{1,0:T(8,128)(2,1)S(1)} %get-tuple-element.2370) | copy-start | bytes 393220
  452.7 6.2 copy-start.5
  452.7 6.2 copy-start.9
  519.4 6.2 copy-start.5
  519.4 6.2 copy-start.9
  652.7 6.2 copy-start.5
  652.8 6.2 copy-start.9
  719.4 6.2 copy-start.5
  854.8 18.4 %all-to-all-start.6 = ((f32[32,8,8]{1,2,0:T(8,128)}), f32[32,8,8]{1,2,0:T(8,128)S(1)}, u32[]{:S(2)}, u32[]{:S(2)}) async-start(f32[32,8,8]{1,2,0:T(8,128)} %copy.135), calls=%async_computation.6 | async-start | bytes 262144 | tf_op jit(solution)/shard_map/all_to_all | solution.py:193
  873.2 14.3 %all-to-all-start.5 = ((f32[32,8,256]{2,1,0:T(8,128)}), f32[32,8,256]{2,1,0:T(8,128)S(1)}, u32[]{:S(2)}, u32[]{:S(2)}) async-start(f32[32,8,256]{2,1,0:T(8,128)} %bitcast.44), calls=%async_computation.5 | async-start | bytes 524288 | tf_op jit(solution)/shard_map/all_to_all | solution.py:195
  887.5 17.0 %all-to-all-start.4 = ((f32[32,8,256]{2,1,0:T(8,128)}), f32[32,8,256]{2,1,0:T(8,128)S(1)}, u32[]{:S(2)}, u32[]{:S(2)}) async-start(f32[32,8,256]{2,1,0:T(8,128)} %bitcast.39), calls=%async_computation.4 | async-start | bytes 524288 | tf_op jit(solution)/shard_map/all_to_all | solution.py:194
  894.8 8.0 collective-permute-start.1
  904.5 20.3 %all-to-all-start.3 = ((bf16[32,8,512]{2,1,0:T(8,128)(2,1)}), bf16[32,8,512]{2,1,0:T(8,128)(2,1)S(1)}, u32[]{:S(2)}, u32[]{:S(2)}) async-start(bf16[32,8,512]{2,1,0:T(8,128)(2,1)} %bitcast.35), calls=%async_computation.3 | async-start | bytes 524288 | tf_op jit(solution)/shard_map/all_to_all | solution.py:189
  (73 other events, 260.5 us)
Sparse Core Ops, SparseCore 0:
  11.2 82.6 all-gather.7
  97.1 79.3 all-gather.9
  178.6 62.1 all-gather.11
  242.8 57.3 all-gather.13
where the time goes:
time: 941 us; the launch traced here: 932 us
  other arithmetic  270 us (29%)
  local copies, waits for them, and re-layouts  240 us (26%)
  waiting for transfers between devices  216 us (23%)
  matrix products  72.4 us (8%)
  starting transfers between devices  63 us (7%)
  loops' own time  33.3 us (4%)
  blocking collectives  22.8 us (2%)
  between operations  14.1 us (1%)
    all_gather x2, waiting for transfers between devices, entering(): everything = jax.tree.map(lambda part: lax.all_gather(part, axis), value)  61.8 us
    all_gather x1, waiting for transfers between devices, shards(): lax.all_gather(b_in, 'head', axis=0, tiled=True)  53.1 us
    select_n x32, other arithmetic, hop(): return jax.tree.map(lambda a, b: jnp.where(reached, a, b), new, before)  52.6 us
    dynamic_update_slice x112, local copies, waits for them, and re-layouts, head_forward(): state_out, outputs = lax.scan(advance, state_in, pieces)  48.8 us
    all_gather x1, waiting for transfers between devices, shards(): lax.all_gather(c_in, 'head', axis=0, tiled=True)  48 us
    another operation x91, other arithmetic  43.5 us
    dynamic_slice x40, local copies, waits for them, and re-layouts, shards(): sums, per_head = lax.scan(head_step, start, inputs)  43.1 us
    another operation x16, loops' own time, head_forward(): state_out, outputs = lax.scan(advance, state_in, pieces)  30.4 us
  transfers between devices with their start and end apart: 13, of which 11 were waited for; matrix products, arithmetic and copies ran while one was open for 6% of the time, Pallas kernels for 0%

commit v1 on v0

v1 whole, which is shorter than its diff:
```python
import functools

import jax
import jax.numpy as jnp
from jax import lax
from jax.experimental import pallas as pl
from jax.experimental.pallas import tpu as pltpu
from jax.sharding import PartitionSpec as P

HEAD_DIM = 64
STATE = 256
GROUPS = 8
CONV = 4
LANES = 128
F32 = jnp.float32
BF16 = jnp.bfloat16


def nn(a, b):
    return lax.dot_general(a, b, (((1,), (0,)), ((), ())), preferred_element_type=F32)


def nt(a, b):
    return lax.dot_general(a, b, (((1,), (1,)), ((), ())), preferred_element_type=F32)


def split(value, pieces=2):
    parts = []
    for _ in range(pieces):
        part = value.astype(BF16)
        parts.append(part)
        value = value - part.astype(F32)
    return parts


def exact_by(dot, exact, wide):
    hi, lo = split(wide)
    return dot(exact, hi) + dot(exact, lo)


def wide_by(dot, wide, exact):
    hi, lo = split(wide)
    return dot(hi, exact) + dot(lo, exact)


def three(dot, left, right):
    lh, ll = split(left)
    rh, rl = split(right)
    return dot(lh, rh) + (dot(lh, rl) + dot(ll, rh))


def expand(cols, width):
    lane = lax.broadcasted_iota(jnp.int32, (cols.shape[0], LANES), 1)
    parts = [
        jnp.where(lane < HEAD_DIM, cols[:, h : h + 1], cols[:, h + 1 : h + 2])
        for h in range(0, width // HEAD_DIM, 2)
    ]
    return jnp.concatenate(parts, axis=1)


def segments(value):
    width = value.shape[1]
    row = lax.broadcasted_iota(jnp.int32, (width, LANES), 0)
    col = lax.broadcasted_iota(jnp.int32, (width, LANES), 1)
    pick = jnp.where(
        (row >= col * HEAD_DIM) & (row < (col + 1) * HEAD_DIM), 1.0, 0.0
    ).astype(BF16)
    return wide_by(nn, value, pick)


def triangle(length, lower):
    row = lax.broadcasted_iota(jnp.int32, (length, length), 0)
    col = lax.broadcasted_iota(jnp.int32, (length, length), 1)
    return row >= col if lower else row <= col


def columns(width):
    x_to = width
    dy_to = 2 * width
    b_to = dy_to + STATE
    c_to = b_to + STATE
    return x_to, dy_to, b_to, c_to


def convolve(rows_ref, edge_ref, par_ref, ext):
    length, width = rows_ref.shape[0], edge_ref.shape[1]
    ext[0:8, :] = edge_ref[...].astype(F32)
    ext[8 : 8 + length, :] = rows_ref[:, 0:width].astype(F32)
    conv = par_ref[4:5, :] + par_ref[0:1, :] * ext[5 : 5 + length, :]
    for k in range(1, CONV):
        conv = conv + par_ref[k : k + 1, :] * ext[5 + k : 5 + k + length, :]
    return conv, 1.0 / (1.0 + jnp.exp(-conv))


def decays(rows_ref, par_ref, width):
    length = rows_ref.shape[0]
    c_to = columns(width)[3]
    dt16 = rows_ref[:, c_to : c_to + LANES]
    lower = jnp.where(triangle(length, True), 1.0, 0.0).astype(BF16)
    rate = par_ref[6:7, 0:LANES]
    return dt16.astype(F32), rate, -rate * nn(lower, dt16)


def states_kernel(parts, rows_ref, edge_ref, par_ref, out_ref, ext):
    length, width = rows_ref.shape[0], edge_ref.shape[1]
    x_to, dy_to, b_to, c_to = columns(width)
    conv, sig = convolve(rows_ref, edge_ref, par_ref, ext)
    activ = conv * sig
    dt, rate, cumul = decays(rows_ref, par_ref, width)
    tail_wt = jnp.exp(cumul[length - 1 : length, :] - cumul) * dt
    grow = expand(jnp.exp(cumul), width)
    b_turned = rows_ref[:, dy_to:b_to].astype(F32).T.astype(BF16)
    c_turned = rows_ref[:, b_to:c_to].astype(F32).T.astype(BF16)
    state = exact_by(nn, b_turned, activ * expand(tail_wt, width))
    pull = exact_by(nn, c_turned, rows_ref[:, x_to:dy_to].astype(F32) * grow)
    piece = STATE // parts
    last = jnp.broadcast_to(grow[length - 1 : length, :], (8, width))
    for j in range(parts):
        out_ref[j, 0:piece, :] = state[j * piece : (j + 1) * piece, :]
        out_ref[j, piece : 2 * piece, :] = pull[j * piece : (j + 1) * piece, :]
        out_ref[j, 2 * piece : 2 * piece + 8, :] = last


def scan_kernel(in_ref, out_ref):
    parts = in_ref.shape[0]
    piece = out_ref.shape[1] // 2
    state = jnp.zeros((piece, in_ref.shape[2]), F32)
    for j in range(parts):
        out_ref[j, 0:piece, :] = state
        state = in_ref[j, 2 * piece : 2 * piece + 1, :] * state + in_ref[j, 0:piece, :]
    state = jnp.zeros((piece, in_ref.shape[2]), F32)
    for j in range(parts - 1, -1, -1):
        out_ref[j, piece : 2 * piece, :] = state
        state = (
            in_ref[j, 2 * piece : 2 * piece + 1, :] * state
            + in_ref[j, piece : 2 * piece, :]
        )


def main_kernel(rows_ref, edge_ref, par_ref, st_ref, out_ref, ends_ref, ext):
    length, width = rows_ref.shape[0], edge_ref.shape[1]
    x_to, dy_to, b_to, c_to = columns(width)
    parts = st_ref.shape[0]
    piece = STATE // parts
    conv, sig = convolve(rows_ref, edge_ref, par_ref, ext)
    activ = conv * sig
    slope = sig * (1.0 + conv * (1.0 - sig))
    dt, rate, cumul = decays(rows_ref, par_ref, width)
    grow = expand(jnp.exp(cumul), width)
    tail = expand(jnp.exp(cumul[length - 1 : length, :] - cumul), width)
    dt_wide = expand(dt, width)
    turned = cumul.T
    dy16 = rows_ref[:, x_to:dy_to]
    dy = dy16.astype(F32)
    b16 = rows_ref[:, dy_to:b_to]
    c16 = rows_ref[:, b_to:c_to]
    state = jnp.concatenate([st_ref[j, 0:piece, :] for j in range(parts)], axis=0)
    pull = jnp.concatenate([st_ref[j, piece : 2 * piece, :] for j in range(parts)], axis=0)
    source = activ * dt_wide

    gram = nt(c16, b16)
    gram_turned = nt(b16, c16)
    lower = triangle(length, True)
    upper = triangle(length, False)
    lane = lax.broadcasted_iota(jnp.int32, (length, LANES), 1)
    g_gram = jnp.zeros((length, length), F32)
    g_cumul = jnp.zeros((length, LANES), F32)
    inner = []
    for pair in range(width // LANES):
        at = slice(pair * LANES, (pair + 1) * LANES)
        src_hi, src_lo = split(source[:, at])
        halves = []
        for side in range(2):
            h = 2 * pair + side
            own = lane < HEAD_DIM if side == 0 else lane >= HEAD_DIM
            dy_own = jnp.where(own, dy[:, at], 0.0).astype(BF16)
            col = cumul[:, h : h + 1]
            row = turned[h : h + 1, :]
            decay = jnp.where(lower, jnp.exp(jnp.minimum(col - row, 0.0)), 0.0)
            inside = decay * (nt(dy_own, src_hi) + nt(dy_own, src_lo))
            g_gram = g_gram + inside
            g_cumul = g_cumul + jnp.where(
                lane == h, jnp.sum(inside * gram, axis=1, keepdims=True), 0.0
            )
            mixing = gram_turned * jnp.where(
                upper, jnp.exp(jnp.minimum(row - col, 0.0)), 0.0
            )
            halves.append(wide_by(nn, mixing, dy16[:, at]))
        inner.append(jnp.where(lane < HEAD_DIM, halves[0], halves[1]))
    pulled = tail * exact_by(nn, b16, pull)
    g_source = jnp.concatenate(inner, axis=1) + pulled

    dy_grown = dy * grow
    direct = segments(activ * g_source)
    g_cumul = g_cumul + segments(dy_grown * exact_by(nn, c16, state)) - dt * direct
    carried = jnp.sum(source * pulled, axis=0, keepdims=True) + grow[
        length - 1 : length, :
    ] * jnp.sum(state * pull, axis=0, keepdims=True)
    carried = segments(jnp.broadcast_to(carried, (16, width)))[0:1, :]
    after = jnp.where(upper, 1.0, 0.0).astype(BF16)
    pieces = split(g_cumul, 3)
    later = nn(after, pieces[0]) + (nn(after, pieces[1]) + nn(after, pieces[2]))
    g_dt = direct - rate * (later + carried)

    g_c = wide_by(nn, g_gram, b16) + three(nt, dy_grown, state)
    g_b = wide_by(nn, g_gram.T, c16) + three(nt, source * tail, pull)

    g_conv = (dt_wide * g_source + expand(par_ref[7:8, 0:LANES], width) * dy) * slope
    ext[0:length, :] = g_conv
    ext[length : length + 8, :] = jnp.zeros((8, width), F32)
    g_x = par_ref[3:4, :] * g_conv
    for k in range(CONV - 1):
        g_x = g_x + par_ref[k : k + 1, :] * ext[CONV - 1 - k : CONV - 1 - k + length, :]
    out_ref[:, 0:width] = g_x.astype(BF16)
    ends_ref[0:8, :] = g_conv[0:8, :]
    ends_ref[8:16, :] = g_x[length - 8 : length, :]
    at = width
    for value in (g_b, g_c):
        for part in split(value):
            out_ref[:, at : at + STATE] = part
            at += STATE
    merged = jnp.zeros((length, LANES), F32)
    for j, part in enumerate(split(g_dt, 3)):
        part = part.astype(F32)
        merged = merged + (pltpu.roll(part, j * (width // HEAD_DIM), 1) if j else part)
    out_ref[:, at : at + LANES] = merged.astype(BF16)


def call(kernel, shapes, scratch, *operands):
    return pl.pallas_call(
        kernel,
        out_shape=shapes,
        in_specs=[pl.BlockSpec(memory_space=pltpu.VMEM)] * len(operands),
        out_specs=jax.tree.map(lambda _: pl.BlockSpec(memory_space=pltpu.VMEM), shapes),
        scratch_shapes=scratch,
        compiler_params=pltpu.CompilerParams(vmem_limit_bytes=56 * 1024 * 1024),
    )(*operands)


def passed_along(value, axis, by):
    count = lax.axis_size(axis)
    pairs = [(i, i + by) for i in range(count) if 0 <= i + by < count]
    return lax.ppermute(value, axis, pairs)


def shards(x_in, grad_y, b_in, c_in, dt, conv_weight, conv_bias, decay_rate, skip):
    n_head = lax.axis_size("head")
    n_ctx = lax.axis_size("ctx")
    per_group = n_head // GROUPS
    tok_dev = x_in.shape[0]
    heads_dev = decay_rate.shape[0]
    width = heads_dev * HEAD_DIM
    length = tok_dev * n_head

    def spread(value):
        value = value.reshape(tok_dev, GROUPS, 1, STATE)
        value = jnp.broadcast_to(value, (tok_dev, GROUPS, per_group, STATE))
        return value.reshape(tok_dev, n_head, STATE)

    sent = jnp.concatenate(
        [
            x_in.reshape(tok_dev, n_head, width),
            grad_y.reshape(tok_dev, n_head, width),
            spread(b_in),
            spread(c_in),
            jnp.pad(
                dt.reshape(tok_dev, n_head, heads_dev),
                ((0, 0), (0, 0), (0, LANES - heads_dev)),
            ),
        ],
        axis=2,
    )
    total = sent.shape[2]
    rows = lax.all_to_all(
        sent.transpose(1, 0, 2), "head", split_axis=0, concat_axis=0, tiled=True
    ).reshape(length, total)
    edge = passed_along(rows[length - 8 :, :width], "ctx", 1)
    wide = lambda value: jnp.pad(value[None, :], ((0, 0), (0, width - heads_dev)))
    params = jnp.concatenate(
        [conv_weight, conv_bias[None, :], conv_bias[None, :], wide(decay_rate), wide(skip)], axis=0
    )
    ext = [pltpu.VMEM((length + 8, width), F32)]
    piece = STATE // n_ctx
    local = call(
        functools.partial(states_kernel, n_ctx),
        jax.ShapeDtypeStruct((n_ctx, 2 * piece + 8, width), F32),
        ext,
        rows,
        edge,
        params,
    )
    local = lax.all_to_all(local, "ctx", split_axis=0, concat_axis=0, tiled=True)
    scanned = call(
        scan_kernel, jax.ShapeDtypeStruct((n_ctx, 2 * piece, width), F32), [], local
    )
    states = lax.all_to_all(scanned, "ctx", split_axis=0, concat_axis=0, tiled=True)
    outs, ends = call(
        main_kernel,
        (
            jax.ShapeDtypeStruct((length, width + 4 * STATE + LANES), BF16),
            jax.ShapeDtypeStruct((16, width), F32),
        ),
        ext,
        rows,
        edge,
        params,
        states,
    )
    first = passed_along(ends[0:8], "ctx", -1)
    tail = ends[8:16]
    for k in range(CONV - 1):
        count = CONV - 1 - k
        tail = tail + jnp.pad(
            conv_weight[k][None, :] * first[0:count], ((8 - count, 0), (0, 0))
        )
    outs = lax.dynamic_update_slice(outs, tail.astype(BF16), (length - 8, 0))
    back = lax.all_to_all(
        outs.reshape(n_head, tok_dev, outs.shape[1]),
        "head",
        split_axis=0,
        concat_axis=0,
        tiled=True,
    )
    grad_x = back[:, :, :width].transpose(1, 0, 2).reshape(tok_dev, n_head * width)

    def gathered(at):
        part = back[:, :, at : at + STATE].astype(F32) + back[
            :, :, at + STATE : at + 2 * STATE
        ].astype(F32)
        part = part.reshape(GROUPS, per_group, tok_dev, STATE).sum(axis=1)
        return part.transpose(1, 0, 2).reshape(tok_dev, GROUPS * STATE).astype(BF16)

    at = width + 4 * STATE
    g_dt = back[:, :, at : at + 3 * heads_dev].astype(F32)
    g_dt = g_dt.reshape(n_head, tok_dev, 3, heads_dev).sum(axis=2)
    grad_dt = g_dt.transpose(1, 0, 2).reshape(tok_dev, n_head * heads_dev)
    return (grad_x, gathered(width), gathered(width + 2 * STATE), grad_dt)


def solution(mesh):
    token = P(("ctx", "head"), None)
    in_specs = (token,) * 5 + (P(None, "head"), P("head"), P("head"), P("head"))
    return jax.shard_map(
        shards, mesh=mesh, in_specs=in_specs, out_specs=(token,) * 4, check_vma=False
    )
```

time: 941 us -> 176 us (0.19)
  other arithmetic: 270 us -> 2.05 us
  local copies, waits for them, and re-layouts: 240 us -> 7.24 us
  waiting for transfers between devices: 216 us -> 3.2 us
  blocking collectives: 22.8 us -> 137 us
  matrix products: 72.4 us -> 0 us
  starting transfers between devices: 63 us -> 11.2 us
  loops' own time: 33.3 us -> 0 us
  Pallas kernels: 0 us -> 13.7 us
  between operations: 14.1 us -> 0.83 us
    all_gather x4 -> x0, waiting for transfers between devices: 163 us -> none  [the longest x2 61.8 us: entering(): everything = jax.tree.map(lambda part: lax.all_gather(part, axis), value)]
    all_to_all x0 -> x4, blocking collectives: none -> 137 us  [the longest x1 46.1 us: shards(): lax.all_to_all(local, 'ctx', split_axis=0, concat_axis=0, tiled=True)]
    dot_general x133 -> x0, matrix products: 72.4 us -> none  [the longest x48 25.2 us: advance(): jnp.dot((act_part * tail_wt[:, None]).T, b_part, precision=HIGH)]
    dynamic_update_slice x136 -> x0, local copies, waits for them, and re-layouts: 65.4 us -> none  [the longest x112 48.8 us: head_forward(): state_out, outputs = lax.scan(advance, state_in, pieces)]
    dynamic_slice x88 -> x0, local copies, waits for them, and re-layouts: 64.7 us -> none  [the longest x40 43.1 us: shards(): sums, per_head = lax.scan(head_step, start, inputs)]
    select_n x32 -> x0, other arithmetic: 52.6 us -> none  [hop(): return jax.tree.map(lambda a, b: jnp.where(reached, a, b), new, before)]
    reduce_sum x66 -> x2, other arithmetic: 51.5 us -> 0.7 us  [the longest x1 0.69 us: gathered(): part = part.reshape(GROUPS, per_group, tok_dev, STATE).sum(axis=1)]
    all_to_all x7 -> x0, starting transfers between devices: 49.1 us -> none  [the longest x1 10.5 us: shards(): lax.all_to_all(dt, 'head', split_axis=1, concat_axis=0, tiled=True)]
  transfers between devices with their start and end apart: 13 -> 2, of which waited for: 11 -> 2; matrix products, arithmetic and copies ran while one was open for 6% -> 0% of each run, Pallas kernels for 0% -> 0%
where the time goes in v1:
time: 176 us; the launch traced here: 175 us
  blocking collectives  137 us (78%)
  Pallas kernels  13.7 us (8%)
  starting transfers between devices  11.2 us (6%)
  local copies, waits for them, and re-layouts  7.24 us (4%)
  waiting for transfers between devices  3.2 us (2%)
  other arithmetic  2.05 us (1%)
    all_to_all x1, blocking collectives, shards(): lax.all_to_all(local, 'ctx', split_axis=0, concat_axis=0, tiled=True)  46.1 us
    all_to_all x1, blocking collectives, shards(): lax.all_to_all(scanned, 'ctx', split_axis=0, concat_axis=0, tiled=True)  32.2 us
    all_to_all x1, blocking collectives, shards(): lax.all_to_all(sent.transpose(1, 0, 2), 'head', split_axis=0, concat_axis...  30.7 us
    all_to_all x1, blocking collectives, shards(): lax.all_to_all(outs.reshape(n_head, tok_dev, outs.shape[1]), 'head', spli...  27.8 us
    pallas_call x3, Pallas kernels, call(): pl.pallas_call(kernel, out_shape=shapes, in_specs=[pl.BlockSpec(memory_sp...  13.7 us
    ppermute x2, starting transfers between devices, passed_along(): return lax.ppermute(value, axis, pairs)  11.2 us
  transfers between devices with their start and end apart: 2, of which 2 were waited for; matrix products, arithmetic and copies ran while one was open for 0% of the time, Pallas kernels for 0%

profile of v1, /device:TPU:1, one launch (start us, length us, event | category | flops | bytes accessed | tf_op | source)
XLA Modules:
  0.0 175.0 jit_solution(14258140188874870310)
XLA Ops:
  0.6 0.8 reshape.59
  1.5 1.0 constant_dynamic-update-slice_fusion.3
  2.5 1.0 constant_dynamic-update-slice_fusion.2
  3.4 0.8 broadcast_in_dim.25
  4.4 30.7 %all_to_all.20 = bf16[32,8,1664]{2,1,0:T(8,128)(2,1)S(1)} all-to-all(bf16[32,8,1664]{2,1,0:T(8,128)(2,1)S(1)} %bitcast.34), channel_id=1, replica_groups=mesh['ctx'=16,'head'=32] {'head'}, dimensions={0} | all-to-all | bytes 1703936 | tf_op jit(solution)/shard_map/all_to_all | solution.py:274
  35.0 9.3 %collective-permute-start = (bf16[8,512]{1,0:T(8,128)(2,1)S(1)}, bf16[8,512]{1,0:T(8,128)(2,1)S(1)}, u32[]{:S(2)}, u32[]{:S(2)}) collective-permute-start(bf16[8,512]{1,0:T(8,128)(2,1)S(1)} %slice.60), channel_id=1, source_target_pairs={{0,32},{32,64},{64,96},{96,128},{128,160},{160,192},{192,224},{224... | collective-permute-start | bytes 24584 | tf_op jit(solution)/shard_map/ppermute | solution.py:243
  44.4 0.6 concatenate.7.par_ref
  45.0 0.1 collective-permute-done.edge_ref
  45.1 0.6 copy-done.1
  45.7 3.8 %shard_map.120 = f32[16,40,512]{2,1,0:T(8,128)} custom-call(bf16[256,1664]{1,0:T(8,128)(2,1)} %bitcast.32, bf16[8,512]{1,0:T(8,128)(2,1)} %copy-done.1, f32[8,512]{1,0:T(8,128)} %concatenate.7.par_ref), custom_call_target="tpu_custom_call" | custom-call | tf_op jit(solution)/shard_map/pallas_call | solution.py:230
  49.5 46.1 %all_to_all.21.in_ref = f32[16,40,512]{2,1,0:T(8,128)} all-to-all(f32[16,40,512]{2,1,0:T(8,128)} %shard_map.120), channel_id=1, replica_groups=mesh['ctx'=16,'head'=32] {'ctx'}, dimensions={0} | all-to-all | bytes 2621440 | tf_op jit(solution)/shard_map/all_to_all | solution.py:292
  95.5 2.4 %shard_map.121 = f32[16,32,512]{2,1,0:T(8,128)} custom-call(f32[16,40,512]{2,1,0:T(8,128)} %all_to_all.21.in_ref), custom_call_target="tpu_custom_call" | custom-call | tf_op jit(solution)/shard_map/pallas_call | solution.py:230
  97.9 32.2 %all_to_all.22.st_ref = f32[16,32,512]{2,1,0:T(8,128)} all-to-all(f32[16,32,512]{2,1,0:T(8,128)} %shard_map.121), channel_id=1, replica_groups=mesh['ctx'=16,'head'=32] {'ctx'}, dimensions={0} | all-to-all | bytes 2097152 | tf_op jit(solution)/shard_map/all_to_all | solution.py:296
  130.2 7.5 %shard_map.122 = (bf16[256,1664]{1,0:T(8,128)(2,1)}, f32[16,512]{1,0:T(8,128)}) custom-call(bf16[256,1664]{1,0:T(8,128)(2,1)} %bitcast.33, bf16[8,512]{1,0:T(8,128)(2,1)} %copy-done.1, f32[8,512]{1,0:T(8,128)} %concatenate.7.par_ref, f32[16,32,512]{2,1,0:T(8,128)} %all_to_all.22.st_ref), custom_call_target="tpu_custom_call" | custom-call | tf_op jit(solution)/shard_map/pallas_call | solution.py:230
  137.7 0.7 slice.48
  138.4 1.9 %collective-permute-start.1 = (f32[8,512]{1,0:T(8,128)S(1)}, f32[8,512]{1,0:T(8,128)S(1)}, u32[]{:S(2)}, u32[]{:S(2)}) collective-permute-start(f32[8,512]{1,0:T(8,128)S(1)} %slice.48), channel_id=1, source_target_pairs={{32,0},{64,32},{96,64},{128,96},{160,128},{192,160},{224,192},{256... | collective-permute-start | bytes 49160 | tf_op jit(solution)/shard_map/ppermute | solution.py:243
  140.3 3.1 %collective-permute-done.1 = f32[8,512]{1,0:T(8,128)S(1)} collective-permute-done((f32[8,512]{1,0:T(8,128)S(1)}, f32[8,512]{1,0:T(8,128)S(1)}, u32[]{:S(2)}, u32[]{:S(2)}) %collective-permute-start.1) | collective-permute-done | bytes 16416 | tf_op jit(solution)/shard_map/ppermute | solution.py:243
  143.4 1.3 fusion
  144.8 27.8 %all_to_all.23 = bf16[32,8,1664]{2,1,0:T(8,128)(2,1)S(1)} all-to-all(bf16[32,8,1664]{2,1,0:T(8,128)(2,1)} %bitcast.35), channel_id=1, replica_groups=mesh['ctx'=16,'head'=32] {'head'}, dimensions={0} | all-to-all | bytes 1703936 | tf_op jit(solution)/shard_map/all_to_all | solution.py:317
  172.6 0.1 copy.30
  172.7 0.1 copy.29
  172.8 0.7 reshape.67
  173.6 0.7 bitcast_reduce_fusion
  174.3 0.7 slice.64
  (26 shorter events, 0.2 us)
Async XLA Ops:
  0.6 3.6 %copy-start.2 = (bf16[8,2048]{1,0:T(8,128)(2,1)S(1)}, bf16[8,2048]{1,0:T(8,128)(2,1)}, u32[]{:S(2)}) copy-start(bf16[8,2048]{1,0:T(8,128)(2,1)} %param.12) | copy-start | bytes 98308
  4.2 40.1 %copy-start.5 = (f32[8]{0:T(128)S(1)}, f32[8]{0:T(128)}, u32[]{:S(2)}) copy-start(f32[8]{0:T(128)} %param.16) | copy-start | bytes 100
  4.2 40.1 %copy-start.6 = (f32[8]{0:T(128)S(1)}, f32[8]{0:T(128)}, u32[]{:S(2)}) copy-start(f32[8]{0:T(128)} %param.17) | copy-start | bytes 100
  4.2 40.1 %copy-start.3 = (f32[4,512]{1,0:T(4,128)S(1)}, f32[4,512]{1,0:T(4,128)}, u32[]{:S(2)}) copy-start(f32[4,512]{1,0:T(4,128)} %param.14) | copy-start | bytes 24580
  4.2 40.1 %copy-start.4 = (f32[512]{0:T(512)S(1)}, f32[512]{0:T(512)}, u32[]{:S(2)}) copy-start(f32[512]{0:T(512)} %param.15) | copy-start | bytes 6148
  35.0 10.0 %copy-start = (bf16[32,8,1664]{2,1,0:T(8,128)(2,1)}, bf16[32,8,1664]{2,1,0:T(8,128)(2,1)S(1)}, u32[]{:S(2)}) copy-start(bf16[32,8,1664]{2,1,0:T(8,128)(2,1)S(1)} %all_to_all.20) | copy-start | bytes 2555908
  35.0 10.0 %collective-permute-start = (bf16[8,512]{1,0:T(8,128)(2,1)S(1)}, bf16[8,512]{1,0:T(8,128)(2,1)S(1)}, u32[]{:S(2)}, u32[]{:S(2)}) collective-permute-start(bf16[8,512]{1,0:T(8,128)(2,1)S(1)} %slice.60), channel_id=1, source_target_pairs={{0,32},{32,64},{64,96},{96,128},{128,160},{160,192},{192,224},{224... | collective-permute-start | bytes 24584 | tf_op jit(solution)/shard_map/ppermute | solution.py:243
  45.1 0.6 copy-start.1
  138.4 5.0 %collective-permute-start.1 = (f32[8,512]{1,0:T(8,128)S(1)}, f32[8,512]{1,0:T(8,128)S(1)}, u32[]{:S(2)}, u32[]{:S(2)}) collective-permute-start(f32[8,512]{1,0:T(8,128)S(1)} %slice.48), channel_id=1, source_target_pairs={{32,0},{64,32},{96,64},{128,96},{160,128},{192,160},{224,192},{256... | collective-permute-start | bytes 49160 | tf_op jit(solution)/shard_map/ppermute | solution.py:243

commit v2 on v1

v2 whole, which is shorter than its diff:
```python
import functools

import jax
import jax.numpy as jnp
from jax import lax
from jax.experimental import pallas as pl
from jax.experimental.pallas import tpu as pltpu
from jax.sharding import PartitionSpec as P

HEAD_DIM = 64
STATE = 256
GROUPS = 8
CONV = 4
LANES = 128
F32 = jnp.float32
BF16 = jnp.bfloat16
MESH = pl.DeviceIdType.MESH
CHUNK = 16


def nn(a, b):
    return lax.dot_general(a, b, (((1,), (0,)), ((), ())), preferred_element_type=F32)


def nt(a, b):
    return lax.dot_general(a, b, (((1,), (1,)), ((), ())), preferred_element_type=F32)


def split(value, pieces=2):
    parts = []
    for _ in range(pieces):
        part = value.astype(BF16)
        parts.append(part)
        value = value - part.astype(F32)
    return parts


def exact_by(dot, exact, wide):
    hi, lo = split(wide)
    return dot(exact, hi) + dot(exact, lo)


def wide_by(dot, wide, exact):
    hi, lo = split(wide)
    return dot(hi, exact) + dot(lo, exact)


def three(dot, left, right):
    lh, ll = split(left)
    rh, rl = split(right)
    return dot(lh, rh) + (dot(lh, rl) + dot(ll, rh))


def expand(cols, width):
    lane = lax.broadcasted_iota(jnp.int32, (cols.shape[0], LANES), 1)
    parts = [
        jnp.where(lane < HEAD_DIM, cols[:, h : h + 1], cols[:, h + 1 : h + 2])
        for h in range(0, width // HEAD_DIM, 2)
    ]
    return jnp.concatenate(parts, axis=1)


def segments(value):
    width = value.shape[1]
    row = lax.broadcasted_iota(jnp.int32, (width, LANES), 0)
    col = lax.broadcasted_iota(jnp.int32, (width, LANES), 1)
    pick = jnp.where(
        (row >= col * HEAD_DIM) & (row < (col + 1) * HEAD_DIM), 1.0, 0.0
    ).astype(BF16)
    return wide_by(nn, value, pick)


def triangle(length, lower):
    row = lax.broadcasted_iota(jnp.int32, (length, length), 0)
    col = lax.broadcasted_iota(jnp.int32, (length, length), 1)
    return row >= col if lower else row <= col


def columns(width):
    x_to = width
    dy_to = 2 * width
    b_to = dy_to + STATE
    c_to = b_to + STATE
    return x_to, dy_to, b_to, c_to


def convolve(rows_ref, par_ref, ext, width):
    length = rows_ref.shape[0]
    ext[8 : 8 + length, :] = rows_ref[:, 0:width].astype(F32)
    conv = par_ref[4:5, :] + par_ref[0:1, :] * ext[5 : 5 + length, :]
    for k in range(1, CONV):
        conv = conv + par_ref[k : k + 1, :] * ext[5 + k : 5 + k + length, :]
    return conv, 1.0 / (1.0 + jnp.exp(-conv))


def decays(rows_ref, par_ref, width):
    length = rows_ref.shape[0]
    c_to = columns(width)[3]
    dt16 = rows_ref[:, c_to : c_to + LANES]
    lower = jnp.where(triangle(length, True), 1.0, 0.0).astype(BF16)
    rate = par_ref[6:7, 0:LANES]
    return dt16.astype(F32), rate, -rate * nn(lower, dt16)


def block_kernel(
    n_ctx,
    rows_ref,
    par_ref,
    out_ref,
    ext,
    edge,
    top_out,
    top_in,
    mine,
    other,
    sib_local,
    decay_own,
    decay_sib,
    chain_in,
    chain_out,
    sib_out,
    sib_in,
    gram_sum,
    cumul_sum,
    inner,
    edge_sems,
    top_sems,
    local_sems,
    decay_sems,
    chain_send,
    chain_recv,
    sib_send,
    sib_recv,
):
    length, width = ext.shape[0] - 8, ext.shape[1]
    x_to, dy_to, b_to, c_to = columns(width)
    me = lax.axis_index("ctx")
    core = lax.rem(me, 2)
    chip = lax.div(me, 2)
    chips = n_ctx // 2
    sign = 1 - 2 * core
    place = core * (chips - 1) + sign * chip
    sibling = me + sign
    ahead = lax.rem(me + 2 * sign + n_ctx, n_ctx)
    following = lax.rem(me + 1, n_ctx)
    leading = lax.rem(me + n_ctx - 1, n_ctx)

    def remote(src, dst, sems, device):
        return pltpu.make_async_remote_copy(
            src_ref=src,
            dst_ref=dst,
            send_sem=sems[0],
            recv_sem=sems[1],
            device_id={"ctx": device},
            device_id_type=MESH,
        )

    barrier = pltpu.get_barrier_semaphore()
    for by in (1, 2, n_ctx - 2, n_ctx - 1):
        pl.semaphore_signal(
            barrier,
            inc=1,
            device_id={"ctx": lax.rem(me + by, n_ctx)},
            device_id_type=MESH,
        )
    pl.semaphore_wait(barrier, 4)

    edge_copy = remote(
        rows_ref.at[length - 16 : length, 0:width],
        edge,
        (edge_sems.at[0], edge_sems.at[1]),
        following,
    )
    edge_copy.start()

    dt, rate, cumul = decays(rows_ref, par_ref, width)
    grow = expand(jnp.exp(cumul), width)
    tail = expand(jnp.exp(cumul[length - 1 : length, :] - cumul), width)
    dt_wide = expand(dt, width)
    dy16 = rows_ref[:, x_to:dy_to]
    dy = dy16.astype(F32)
    b16 = rows_ref[:, dy_to:b_to]
    c16 = rows_ref[:, b_to:c_to]
    b_turned = b16.astype(F32).T.astype(BF16)
    c_turned = c16.astype(F32).T.astype(BF16)
    decay_own[...] = jnp.broadcast_to(grow[length - 1 : length, :], (8, width))
    decay_copy = remote(
        decay_own, decay_sib, (decay_sems.at[0], decay_sems.at[1]), sibling
    )
    decay_copy.start()
    dy_grown = dy * grow
    pull = exact_by(nn, c_turned, dy_grown)

    edge_copy.wait()
    ext[0:8, :] = jnp.where(me > 0, edge[...].astype(F32)[8:16, :], 0.0)
    conv, sig = convolve(rows_ref, par_ref, ext, width)
    activ = conv * sig
    slope = sig * (1.0 + conv * (1.0 - sig))
    source = activ * dt_wide
    state = exact_by(nn, b_turned, source * tail)
    first_core = core == 0
    other[...] = jnp.where(first_core, pull, state)
    mine[...] = jnp.where(first_core, state, pull)
    local_copy = remote(
        other, sib_local, (local_sems.at[0], local_sems.at[1]), sibling
    )
    local_copy.start()

    lower = triangle(length, True)
    upper = triangle(length, False)
    lane = lax.broadcasted_iota(jnp.int32, (length, LANES), 1)

    def within():
        turned = cumul.T
        gram = nt(c16, b16)
        gram_turned = nt(b16, c16)
        g_gram = jnp.zeros((length, length), F32)
        g_cumul = jnp.zeros((length, LANES), F32)
        for pair in range(width // LANES):
            at = slice(pair * LANES, (pair + 1) * LANES)
            src_hi, src_lo = split(source[:, at])
            halves = []
            for side in range(2):
                h = 2 * pair + side
                own = lane < HEAD_DIM if side == 0 else lane >= HEAD_DIM
                dy_own = jnp.where(own, dy[:, at], 0.0).astype(BF16)
                col = cumul[:, h : h + 1]
                row = turned[h : h + 1, :]
                decay = jnp.where(lower, jnp.exp(jnp.minimum(col - row, 0.0)), 0.0)
                inside = decay * (nt(dy_own, src_hi) + nt(dy_own, src_lo))
                g_gram = g_gram + inside
                g_cumul = g_cumul + jnp.where(
                    lane == h, jnp.sum(inside * gram, axis=1, keepdims=True), 0.0
                )
                mixing = gram_turned * jnp.where(
                    upper, jnp.exp(jnp.minimum(row - col, 0.0)), 0.0
                )
                halves.append(wide_by(nn, mixing, dy16[:, at]))
            inner[:, at] = jnp.where(lane < HEAD_DIM, halves[0], halves[1])
        gram_sum[...] = g_gram
        cumul_sum[...] = g_cumul

    late = place >= (chips + 1) // 2

    @pl.when(place == 0)
    def _():
        chain_in[...] = jnp.zeros_like(chain_in)

    decay_copy.wait()
    local_copy.wait()

    @pl.when(late)
    def _():
        within()

    def chain_copy(c):
        rows = pl.ds(pl.multiple_of(c * CHUNK, CHUNK), CHUNK)
        return remote(
            chain_out.at[rows, :],
            chain_in.at[rows, :],
            (chain_send.at[c], chain_recv.at[c]),
            ahead,
        )

    def sib_copy(c):
        rows = pl.ds(pl.multiple_of(c * CHUNK, CHUNK), CHUNK)
        return remote(
            sib_out.at[rows, :],
            sib_in.at[rows, :],
            (sib_send.at[c], sib_recv.at[c]),
            sibling,
        )

    def hop(c, _):
        rows = pl.ds(pl.multiple_of(c * CHUNK, CHUNK), CHUNK)

        @pl.when(place > 0)
        def _():
            chain_copy(c).wait_recv()

        here = decay_own[0:1, :] * chain_in[rows, :] + mine[rows, :]
        chain_out[rows, :] = decay_sib[0:1, :] * here + sib_local[rows, :]

        @pl.when(place < chips - 1)
        def _():
            chain_copy(c).start()

        sib_out[rows, :] = here
        sib_copy(c).start()
        return 0

    chunks = STATE // CHUNK
    lax.fori_loop(0, chunks, hop, 0)

    @pl.when(jnp.logical_not(late))
    def _():
        within()

    def drain(c, _):
        @pl.when(place < chips - 1)
        def _():
            chain_copy(c).wait_send()

        sib_copy(c).wait()
        return 0

    lax.fori_loop(0, chunks, drain, 0)

    state = jnp.where(first_core, chain_in[...], sib_in[...])
    pull = jnp.where(first_core, sib_in[...], chain_in[...])
    pulled = tail * exact_by(nn, b16, pull)
    g_source = inner[...] + pulled
    g_conv = (dt_wide * g_source + expand(par_ref[7:8, 0:LANES], width) * dy) * slope
    ext[0:length, :] = g_conv
    top_out[...] = g_conv[0:8, :]
    top_copy = remote(top_out, top_in, (top_sems.at[0], top_sems.at[1]), leading)
    top_copy.start()

    direct = segments(activ * g_source)
    g_cumul = (
        cumul_sum[...] + segments(dy_grown * exact_by(nn, c16, state)) - dt * direct
    )
    carried = jnp.sum(source * pulled, axis=0, keepdims=True) + grow[
        length - 1 : length, :
    ] * jnp.sum(state * pull, axis=0, keepdims=True)
    carried = segments(jnp.broadcast_to(carried, (16, width)))[0:1, :]
    after = jnp.where(upper, 1.0, 0.0).astype(BF16)
    pieces = split(g_cumul, 3)
    later = nn(after, pieces[0]) + (nn(after, pieces[1]) + nn(after, pieces[2]))
    g_dt = direct - rate * (later + carried)
    g_gram = gram_sum[...]
    g_c = wide_by(nn, g_gram, b16) + three(nt, dy_grown, state)
    g_b = wide_by(nn, g_gram.T, c16) + three(nt, source * tail, pull)
    at = width
    for value in (g_b, g_c):
        for part in split(value):
            out_ref[:, at : at + STATE] = part
            at += STATE
    merged = jnp.zeros((length, LANES), F32)
    for j, part in enumerate(split(g_dt, 3)):
        part = part.astype(F32)
        merged = merged + (pltpu.roll(part, j * (width // HEAD_DIM), 1) if j else part)
    out_ref[:, at : at + LANES] = merged.astype(BF16)

    top_copy.wait()
    ext[length : length + 8, :] = jnp.where(me < n_ctx - 1, top_in[...], 0.0)
    g_x = par_ref[3:4, :] * g_conv
    for k in range(CONV - 1):
        g_x = g_x + par_ref[k : k + 1, :] * ext[CONV - 1 - k : CONV - 1 - k + length, :]
    out_ref[:, 0:width] = g_x.astype(BF16)


def shards(x_in, grad_y, b_in, c_in, dt, conv_weight, conv_bias, decay_rate, skip):
    n_head = lax.axis_size("head")
    n_ctx = lax.axis_size("ctx")
    per_group = n_head // GROUPS
    tok_dev = x_in.shape[0]
    heads_dev = decay_rate.shape[0]
    width = heads_dev * HEAD_DIM
    length = tok_dev * n_head

    def spread(value):
        value = value.reshape(tok_dev, GROUPS, 1, STATE)
        value = jnp.broadcast_to(value, (tok_dev, GROUPS, per_group, STATE))
        return value.reshape(tok_dev, n_head, STATE)

    sent = jnp.concatenate(
        [
            x_in.reshape(tok_dev, n_head, width),
            grad_y.reshape(tok_dev, n_head, width),
            spread(b_in),
            spread(c_in),
            jnp.pad(
                dt.reshape(tok_dev, n_head, heads_dev),
                ((0, 0), (0, 0), (0, LANES - heads_dev)),
            ),
        ],
        axis=2,
    )
    total = sent.shape[2]
    rows = lax.all_to_all(
        sent.transpose(1, 0, 2), "head", split_axis=0, concat_axis=0, tiled=True
    ).reshape(length, total)
    wide = lambda value: jnp.pad(value[None, :], ((0, 0), (0, width - heads_dev)))
    params = jnp.concatenate(
        [conv_weight, conv_bias[None, :], conv_bias[None, :], wide(decay_rate), wide(skip)], axis=0
    )
    whole = pltpu.VMEM((STATE, width), F32)
    small = pltpu.VMEM((8, width), F32)
    pair = pltpu.SemaphoreType.DMA((2,))
    many = pltpu.SemaphoreType.DMA((STATE // CHUNK,))
    outs = pl.pallas_call(
        functools.partial(block_kernel, n_ctx),
        out_shape=jax.ShapeDtypeStruct((length, width + 4 * STATE + LANES), BF16),
        in_specs=[pl.BlockSpec(memory_space=pltpu.VMEM)] * 2,
        out_specs=pl.BlockSpec(memory_space=pltpu.VMEM),
        scratch_shapes=[
            pltpu.VMEM((length + 8, width), F32),
            pltpu.VMEM((16, width), BF16),
            small,
            small,
            whole,
            whole,
            whole,
            small,
            small,
            whole,
            whole,
            whole,
            whole,
            pltpu.VMEM((length, length), F32),
            pltpu.VMEM((length, LANES), F32),
            pltpu.VMEM((length, width), F32),
            pair,
            pair,
            pair,
            pair,
            many,
            many,
            many,
            many,
        ],
        compiler_params=pltpu.CompilerParams(
            vmem_limit_bytes=56 * 1024 * 1024, collective_id=0, has_side_effects=True
        ),
    )(rows, params)
    back = lax.all_to_all(
        outs.reshape(n_head, tok_dev, outs.shape[1]),
        "head",
        split_axis=0,
        concat_axis=0,
        tiled=True,
    )
    grad_x = back[:, :, :width].transpose(1, 0, 2).reshape(tok_dev, n_head * width)

    def gathered(at):
        part = back[:, :, at : at + STATE].astype(F32) + back[
            :, :, at + STATE : at + 2 * STATE
        ].astype(F32)
        part = part.reshape(GROUPS, per_group, tok_dev, STATE).sum(axis=1)
        return part.transpose(1, 0, 2).reshape(tok_dev, GROUPS * STATE).astype(BF16)

    at = width + 4 * STATE
    g_dt = back[:, :, at : at + 3 * heads_dev].astype(F32)
    g_dt = g_dt.reshape(n_head, tok_dev, 3, heads_dev).sum(axis=2)
    grad_dt = g_dt.transpose(1, 0, 2).reshape(tok_dev, n_head * heads_dev)
    return (grad_x, gathered(width), gathered(width + 2 * STATE), grad_dt)


def solution(mesh):
    token = P(("ctx", "head"), None)
    in_specs = (token,) * 5 + (P(None, "head"), P("head"), P("head"), P("head"))
    return jax.shard_map(
        shards, mesh=mesh, in_specs=in_specs, out_specs=(token,) * 4, check_vma=False
    )
```

time: 176 us -> 115 us (0.65)
  the two profiles are of different devices: /device:TPU:1 before, /device:TPU:8 now
where the time goes in v2:
time: 115 us; the launch traced here: 114 us
  Pallas kernels  41.3 us (36%)
  blocking collectives  29.4 us (26%)
  waiting for transfers between devices  23.2 us (20%)
  starting transfers between devices  10.3 us (9%)
  local copies, waits for them, and re-layouts  8.6 us (7%)
    pallas_call x1, Pallas kernels, shards(): pl.pallas_call(functools.partial(block_kernel, n_ctx), out_shape=jax.Shap...  41.3 us
    all_to_all x1, blocking collectives, shards(): lax.all_to_all(outs.reshape(n_head, tok_dev, outs.shape[1]), 'head', spli...  29.4 us
    all_to_all x1, waiting for transfers between devices, shards(): lax.all_to_all(sent.transpose(1, 0, 2), 'head', split_axis=0, concat_axis...  23.2 us
    all_to_all x1, starting transfers between devices, shards(): lax.all_to_all(sent.transpose(1, 0, 2), 'head', split_axis=0, concat_axis...  10.3 us
    unnamed x24, local copies, waits for them, and re-layouts  5.65 us
  transfers between devices with their start and end apart: 1, of which 1 were waited for; matrix products, arithmetic and copies ran while one was open for 1% of the time, Pallas kernels for 0%

profile of v2, /device:TPU:8, one launch (start us, length us, event | category | flops | bytes accessed | tf_op | source)
XLA Modules:
  0.0 114.2 jit_solution(13259292972315645377)
XLA Ops:
  0.7 1.7 %constant_dynamic-update-slice_fusion.3 = bf16[8,32,1664]{2,0,1:T(8,128)(2,1)} fusion(bf16[8,32,512]{2,0,1:T(8,128)(2,1)} %bitcast.33), kind=kLoop, calls=%fused_computation.9 | loop fusion | bytes 524288
  2.4 0.1 reshape.59
  2.5 0.0 copy-start.2
  2.6 0.7 constant_dynamic-update-slice_fusion.2
  3.3 0.0 copy-done.2
  3.3 0.0 copy-start.3
  3.3 0.7 constant_dynamic-update-slice_fusion.1
  4.0 0.1 copy-done.3
  4.1 0.7 constant_dynamic-update-slice_fusion
  4.8 0.6 pad_dynamic-update-slice_fusion
  5.4 10.3 %all-to-all-start = ((bf16[32,8,1664]{2,1,0:T(8,128)(2,1)}), bf16[32,8,1664]{2,1,0:T(8,128)(2,1)S(1)}, u32[]{:S(2)}, u32[]{:S(2)}) async-start(bf16[32,8,1664]{2,1,0:T(8,128)(2,1)} %bitcast.6), calls=%async_computation | async-start | bytes 1703936 | tf_op jit(solution)/shard_map/all_to_all | solution.py:381
  15.7 0.0 copy-start.5
  15.8 0.6 copy-done.5
  16.4 0.0 copy-done.4
  16.5 0.6 concatenate.7.par_ref
  17.1 23.2 %all-to-all-done = bf16[32,8,1664]{2,1,0:T(8,128)(2,1)S(1)} async-done(((bf16[32,8,1664]{2,1,0:T(8,128)(2,1)}), bf16[32,8,1664]{2,1,0:T(8,128)(2,1)S(1)}, u32[]{:S(2)}, u32[]{:S(2)}) %all-to-all-start) | async-done | bytes 852000 | tf_op jit(solution)/shard_map/all_to_all | solution.py:381
  40.3 0.9 copy-done
  41.2 41.3 %shard_map.120 = bf16[256,1664]{1,0:T(8,128)(2,1)} custom-call(bf16[256,1664]{1,0:T(8,128)(2,1)} %bitcast.29, f32[8,512]{1,0:T(8,128)} %concatenate.7.par_ref), custom_call_target="tpu_custom_call" | custom-call | tf_op jit(solution)/shard_map/pallas_call | solution.py:392
  82.4 29.4 %all_to_all.10 = bf16[32,8,1664]{2,1,0:T(8,128)(2,1)S(1)} all-to-all(bf16[32,8,1664]{2,1,0:T(8,128)(2,1)} %bitcast.30), channel_id=1, replica_groups=mesh['ctx'=16,'head'=32] {'head'}, dimensions={0} | all-to-all | bytes 1703936 | tf_op jit(solution)/shard_map/all_to_all | solution.py:427
  111.8 0.1 copy.30
  111.9 0.1 copy.29
  112.0 0.7 reshape.67
  112.8 0.7 bitcast_reduce_fusion
  113.4 0.7 slice.24
  (17 shorter events, 0.1 us)
Async XLA Ops:
  0.6 1.7 %copy-start.6 = (bf16[8,256]{1,0:T(8,128)(2,1)S(1)}, bf16[8,256]{1,0:T(8,128)(2,1)}, u32[]{:S(2)}) copy-start(bf16[8,256]{1,0:T(8,128)(2,1)} %param.13) | copy-start | bytes 12292
  0.6 1.9 %copy-start.1 = (bf16[8,16384]{1,0:T(8,128)(2,1)S(1)}, bf16[8,16384]{1,0:T(8,128)(2,1)}, u32[]{:S(2)}) copy-start(bf16[8,16384]{1,0:T(8,128)(2,1)} %param.10) | copy-start | bytes 786436
  2.5 0.8 copy-start.2
  3.3 0.8 copy-start.3
  5.4 10.3 %copy-start.7 = (f32[8]{0:T(128)S(1)}, f32[8]{0:T(128)}, u32[]{:S(2)}) copy-start(f32[8]{0:T(128)} %param.16) | copy-start | bytes 100
  5.4 10.3 %copy-start.8 = (f32[8]{0:T(128)S(1)}, f32[8]{0:T(128)}, u32[]{:S(2)}) copy-start(f32[8]{0:T(128)} %param.17) | copy-start | bytes 100
  5.4 34.8 %all-to-all-start = ((bf16[32,8,1664]{2,1,0:T(8,128)(2,1)}), bf16[32,8,1664]{2,1,0:T(8,128)(2,1)S(1)}, u32[]{:S(2)}, u32[]{:S(2)}) async-start(bf16[32,8,1664]{2,1,0:T(8,128)(2,1)} %bitcast.6), calls=%async_computation | async-start | bytes 1703936 | tf_op jit(solution)/shard_map/all_to_all | solution.py:381
  15.7 0.7 copy-start.5
  15.8 0.7 copy-start.4
  40.3 0.9 copy-start

commit v3 on v2

--- a/solution.py
+++ b/solution.py
@@ -76,37 +76,47 @@
     return row >= col if lower else row <= col
 
 
-def columns(width):
-    x_to = width
-    dy_to = 2 * width
-    b_to = dy_to + STATE
-    c_to = b_to + STATE
-    return x_to, dy_to, b_to, c_to
-
-
-def convolve(rows_ref, par_ref, ext, width):
-    length = rows_ref.shape[0]
-    ext[8 : 8 + length, :] = rows_ref[:, 0:width].astype(F32)
+def convolve(x, par_ref, ext):
+    length = x.shape[0]
+    ext[8 : 8 + length, :] = x
     conv = par_ref[4:5, :] + par_ref[0:1, :] * ext[5 : 5 + length, :]
     for k in range(1, CONV):
         conv = conv + par_ref[k : k + 1, :] * ext[5 + k : 5 + k + length, :]
     return conv, 1.0 / (1.0 + jnp.exp(-conv))
 
 
-def decays(rows_ref, par_ref, width):
-    length = rows_ref.shape[0]
-    c_to = columns(width)[3]
-    dt16 = rows_ref[:, c_to : c_to + LANES]
-    lower = jnp.where(triangle(length, True), 1.0, 0.0).astype(BF16)
-    rate = par_ref[6:7, 0:LANES]
-    return dt16.astype(F32), rate, -rate * nn(lower, dt16)
+def flat(ref):
+    value = ref[...].astype(F32)
+    return value.reshape(value.shape[0] * value.shape[1], value.shape[2])
 
 
 def block_kernel(
     n_ctx,
-    rows_ref,
+    n_head,
+    x_ref,
+    dy_ref,
+    b_ref,
+    c_ref,
+    dt_ref,
     par_ref,
-    out_ref,
+    gx_ref,
+    gb_ref,
+    gc_ref,
+    gdt_ref,
+    x_buf,
+    dy_buf,
+    b_buf,
+    c_buf,
+    dt_buf,
+    gx_buf,
+    gb_buf,
+    gc_buf,
+    gdt_buf,
+    gb_all,
+    gc_all,
+    gdt_all,
+    head_send,
+    head_recv,
     ext,
     edge,
     top_out,
@@ -133,7 +143,11 @@
     sib_recv,
 ):
     length, width = ext.shape[0] - 8, ext.shape[1]
-    x_to, dy_to, b_to, c_to = columns(width)
+    tok_dev = x_ref.shape[0]
+    heads_dev = width // HEAD_DIM
+    per_group = n_head // GROUPS
+    per_tile = LANES // heads_dev
+    head = lax.axis_index("head")
     me = lax.axis_index("ctx")
     core = lax.rem(me, 2)
     chip = lax.div(me, 2)
@@ -145,13 +159,13 @@
     following = lax.rem(me + 1, n_ctx)
     leading = lax.rem(me + n_ctx - 1, n_ctx)
 
-    def remote(src, dst, sems, device):
+    def remote(src, dst, sems, device, axis="ctx"):
         return pltpu.make_async_remote_copy(
             src_ref=src,
             dst_ref=dst,
             send_sem=sems[0],
             recv_sem=sems[1],
-            device_id={"ctx": device},
+            device_id={axis: device},
             device_id_type=MESH,
         )
 
@@ -163,37 +177,87 @@
             device_id={"ctx": lax.rem(me + by, n_ctx)},
             device_id_type=MESH,
         )
-    pl.semaphore_wait(barrier, 4)
-
+
+    def greet(k, _):
+        pl.semaphore_signal(
+            barrier,
+            inc=1,
+            device_id={"head": lax.rem(head + k, n_head)},
+            device_id_type=MESH,
+        )
+        return 0
+
+    lax.fori_loop(1, n_head, greet, 0)
+    pl.semaphore_wait(barrier, 3 + n_head)
+
+    def scatter(kind, source, target):
+        def step(k, _):
+            to = lax.rem(head + k, n_head)
+            remote(
+                source(to), target, (head_send.at[kind], head_recv.at[kind]), to, "head"
+            ).start()
+            return 0
+
+        lax.fori_loop(1, n_head, step, 0)
+        pltpu.make_async_copy(source(head), target, head_recv.at[kind]).start()
+
+    def arrived(kind, buffer):
+        pltpu.make_async_copy(buffer, buffer, head_recv.at[kind]).wait()
+
+    def sent(kind, buffer):
+        part = buffer.at[0 : n_head - 1]
+        pltpu.make_async_copy(part, part, head_send.at[kind]).wait()
+
+    def lanes(ref, start, size):
+        return ref.at[:, pl.ds(pl.multiple_of(start, LANES), size)]
+
+    scatter(0, lambda to: lanes(b_ref, lax.div(to, per_group) * STATE, STATE), b_buf.at[head])
+    scatter(1, lambda to: lanes(c_ref, lax.div(to, per_group) * STATE, STATE), c_buf.at[head])
+    scatter(2, lambda to: lanes(dt_ref, lax.div(to, per_tile) * LANES, LANES), dt_buf.at[head])
+    scatter(3, lambda to: lanes(x_ref, to * width, width), x_buf.at[head])
+    scatter(4, lambda to: lanes(dy_ref, to * width, width), dy_buf.at[head])
+
+    lower = triangle(length, True)
+    upper = triangle(length, False)
+    lane = lax.broadcasted_iota(jnp.int32, (length, LANES), 1)
+    arrived(0, b_buf)
+    arrived(1, c_buf)
+    arrived(2, dt_buf)
+    shift = lax.rem(LANES - lax.rem(head, per_tile) * heads_dev, LANES)
+    dt = jnp.where(lane < heads_dev, pltpu.roll(flat(dt_buf), shift, 1), 0.0)
+    rate = par_ref[6:7, 0:LANES]
+    cumul = -rate * nn(jnp.where(lower, 1.0, 0.0).astype(BF16), dt.astype(BF16))
+    grow = expand(jnp.exp(cumul), width)
+    tail = expand(jnp.exp(cumul[length - 1 : length, :] - cumul), width)
+    dt_wide = expand(dt, width)
+    b32 = flat(b_buf)
+    c32 = flat(c_buf)
+    b16 = b32.astype(BF16)
+    c16 = c32.astype(BF16)
+    b_turned = b32.T.astype(BF16)
+    c_turned = c32.T.astype(BF16)
+    decay_own[...] = jnp.broadcast_to(grow[length - 1 : length, :], (8, width))
+    decay_copy = remote(
+        decay_own, decay_sib, (decay_sems.at[0], decay_sems.at[1]), sibling
+    )
+    decay_copy.start()
+    arrived(3, x_buf)
     edge_copy = remote(
-        rows_ref.at[length - 16 : length, 0:width],
+        x_buf.at[n_head - 1, tok_dev - 8 : tok_dev, :],
         edge,
         (edge_sems.at[0], edge_sems.at[1]),
         following,
     )
     edge_copy.start()
-
-    dt, rate, cumul = decays(rows_ref, par_ref, width)
-    grow = expand(jnp.exp(cumul), width)
-    tail = expand(jnp.exp(cumul[length - 1 : length, :] - cumul), width)
-    dt_wide = expand(dt, width)
-    dy16 = rows_ref[:, x_to:dy_to]
-    dy = dy16.astype(F32)
-    b16 = rows_ref[:, dy_to:b_to]
-    c16 = rows_ref[:, b_to:c_to]
-    b_turned = b16.astype(F32).T.astype(BF16)
-    c_turned = c16.astype(F32).T.astype(BF16)
-    decay_own[...] = jnp.broadcast_to(grow[length - 1 : length, :], (8, width))
-    decay_copy = remote(
-        decay_own, decay_sib, (decay_sems.at[0], decay_sems.at[1]), sibling
-    )
-    decay_copy.start()
+    arrived(4, dy_buf)
+    dy = flat(dy_buf)
+    dy16 = dy.astype(BF16)
     dy_grown = dy * grow
     pull = exact_by(nn, c_turned, dy_grown)
 
     edge_copy.wait()
-    ext[0:8, :] = jnp.where(me > 0, edge[...].astype(F32)[8:16, :], 0.0)
-    conv, sig = convolve(rows_ref, par_ref, ext, width)
+    ext[0:8, :] = jnp.where(me > 0, edge[...].astype(F32), 0.0)
+    conv, sig = convolve(flat(x_buf), par_ref, ext)
     activ = conv * sig
     slope = sig * (1.0 + conv * (1.0 - sig))
     source = activ * dt_wide
@@ -205,10 +269,6 @@
         other, sib_local, (local_sems.at[0], local_sems.at[1]), sibling
     )
     local_copy.start()
-
-    lower = triangle(length, True)
-    upper = triangle(length, False)
-    lane = lax.broadcasted_iota(jnp.int32, (length, LANES), 1)
 
     def within():
         turned = cumul.T
@@ -316,6 +376,25 @@
     top_copy = remote(top_out, top_in, (top_sems.at[0], top_sems.at[1]), leading)
     top_copy.start()
 
+    def by_token(value):
+        return value.reshape(n_head, tok_dev, value.shape[1])
+
+    g_gram = gram_sum[...]
+    gb_buf[...] = by_token(
+        wide_by(nn, g_gram.T, c16) + three(nt, source * tail, pull)
+    )
+    scatter(5, lambda to: gb_buf.at[to], gb_all.at[head])
+    gc_buf[...] = by_token(wide_by(nn, g_gram, b16) + three(nt, dy_grown, state))
+    scatter(6, lambda to: gc_buf.at[to], gc_all.at[head])
+
+    top_copy.wait()
+    ext[length : length + 8, :] = jnp.where(me < n_ctx - 1, top_in[...], 0.0)
+    g_x = par_ref[3:4, :] * g_conv
+    for k in range(CONV - 1):
+        g_x = g_x + par_ref[k : k + 1, :] * ext[CONV - 1 - k : CONV - 1 - k + length, :]
+    gx_buf[...] = by_token(g_x).astype(BF16)
+    scatter(7, lambda to: gx_buf.at[to], lanes(gx_ref, head * width, width))
+
     direct = segments(activ * g_source)
     g_cumul = (
         cumul_sum[...] + segments(dy_grown * exact_by(nn, c16, state)) - dt * direct
@@ -328,26 +407,39 @@
     pieces = split(g_cumul, 3)
     later = nn(after, pieces[0]) + (nn(after, pieces[1]) + nn(after, pieces[2]))
     g_dt = direct - rate * (later + carried)
-    g_gram = gram_sum[...]
-    g_c = wide_by(nn, g_gram, b16) + three(nt, dy_grown, state)
-    g_b = wide_by(nn, g_gram.T, c16) + three(nt, source * tail, pull)
-    at = width
-    for value in (g_b, g_c):
-        for part in split(value):
-            out_ref[:, at : at + STATE] = part
-            at += STATE
     merged = jnp.zeros((length, LANES), F32)
     for j, part in enumerate(split(g_dt, 3)):
         part = part.astype(F32)
-        merged = merged + (pltpu.roll(part, j * (width // HEAD_DIM), 1) if j else part)
-    out_ref[:, at : at + LANES] = merged.astype(BF16)
-
-    top_copy.wait()
-    ext[length : length + 8, :] = jnp.where(me < n_ctx - 1, top_in[...], 0.0)
-    g_x = par_ref[3:4, :] * g_conv
-    for k in range(CONV - 1):
-        g_x = g_x + par_ref[k : k + 1, :] * ext[CONV - 1 - k : CONV - 1 - k + length, :]
-    out_ref[:, 0:width] = g_x.astype(BF16)
+        merged = merged + (pltpu.roll(part, j * heads_dev, 1) if j else part)
+    gdt_buf[...] = by_token(merged).astype(BF16)
+    scatter(8, lambda to: gdt_buf.at[to], gdt_all.at[head])
+
+    for kind, buffer, result in ((5, gb_all, gb_ref), (6, gc_all, gc_ref)):
+        arrived(kind, buffer)
+        for g in range(GROUPS):
+            summed = buffer[g * per_group]
+            for j in range(1, per_group):
+                summed = summed + buffer[g * per_group + j]
+            result[:, g * STATE : (g + 1) * STATE] = summed.astype(BF16)
+    arrived(8, gdt_all)
+    own = lax.broadcasted_iota(jnp.int32, (tok_dev, LANES), 1) < heads_dev
+    for tile in range(n_head // per_tile):
+        summed = jnp.zeros((tok_dev, LANES), F32)
+        for j in range(per_tile):
+            value = gdt_all[tile * per_tile + j].astype(F32)
+            value = (
+                value
+                + pltpu.roll(value, LANES - heads_dev, 1)
+                + pltpu.roll(value, LANES - 2 * heads_dev, 1)
+            )
+            value = jnp.where(own, value, 0.0)
+            summed = summed + (pltpu.roll(value, j * heads_dev, 1) if j else value)
+        gdt_ref[:, tile * LANES : (tile + 1) * LANES] = summed
+    arrived(7, gx_ref)
+    for kind, buffer in enumerate(
+        (b_buf, c_buf, dt_buf, x_buf, dy_buf, gb_buf, gc_buf, gx_buf, gdt_buf)
+    ):
+        sent(kind, buffer)
 
 
 def shards(x_in, grad_y, b_in, c_in, dt, conv_weight, conv_bias, decay_rate, skip):
@@ -359,44 +451,42 @@
     width = heads_dev * HEAD_DIM
     length = tok_dev * n_head
 
-    def spread(value):
-        value = value.reshape(tok_dev, GROUPS, 1, STATE)
-        value = jnp.broadcast_to(value, (tok_dev, GROUPS, per_group, STATE))
-        return value.reshape(tok_dev, n_head, STATE)
-
-    sent = jnp.concatenate(
-        [
-            x_in.reshape(tok_dev, n_head, width),
-            grad_y.reshape(tok_dev, n_head, width),
-            spread(b_in),
-            spread(c_in),
-            jnp.pad(
-                dt.reshape(tok_dev, n_head, heads_dev),
-                ((0, 0), (0, 0), (0, LANES - heads_dev)),
-            ),
-        ],
-        axis=2,
-    )
-    total = sent.shape[2]
-    rows = lax.all_to_all(
-        sent.transpose(1, 0, 2), "head", split_axis=0, concat_axis=0, tiled=True
-    ).reshape(length, total)
     wide = lambda value: jnp.pad(value[None, :], ((0, 0), (0, width - heads_dev)))
     params = jnp.concatenate(
         [conv_weight, conv_bias[None, :], conv_bias[None, :], wide(decay_rate), wide(skip)], axis=0
     )
     whole = pltpu.VMEM((STATE, width), F32)
     small = pltpu.VMEM((8, width), F32)
+    held = lambda size, kind: pltpu.VMEM((n_head, tok_dev, size), kind)
     pair = pltpu.SemaphoreType.DMA((2,))
     many = pltpu.SemaphoreType.DMA((STATE // CHUNK,))
-    outs = pl.pallas_call(
-        functools.partial(block_kernel, n_ctx),
-        out_shape=jax.ShapeDtypeStruct((length, width + 4 * STATE + LANES), BF16),
-        in_specs=[pl.BlockSpec(memory_space=pltpu.VMEM)] * 2,
-        out_specs=pl.BlockSpec(memory_space=pltpu.VMEM),
+    return pl.pallas_call(
+        functools.partial(block_kernel, n_ctx, n_head),
+        out_shape=(
+            jax.ShapeDtypeStruct(x_in.shape, BF16),
+            jax.ShapeDtypeStruct(b_in.shape, BF16),
+            jax.ShapeDtypeStruct(c_in.shape, BF16),
+            jax.ShapeDtypeStruct(dt.shape, F32),
+        ),
+        in_specs=[pl.BlockSpec(memory_space=pltpu.VMEM)] * 6,
+        out_specs=[pl.BlockSpec(memory_space=pltpu.VMEM)] * 4,
         scratch_shapes=[
+            held(width, BF16),
+            held(width, BF16),
+            held(STATE, BF16),
+            held(STATE, BF16),
+            held(LANES, BF16),
+            held(width, BF16),
+            held(STATE, F32),
+            held(STATE, F32),
+            held(LANES, BF16),
+            held(STATE, F32),
+            held(STATE, F32),
+            held(LANES, BF16),
+            pltpu.SemaphoreType.DMA((9,)),
+            pltpu.SemaphoreType.DMA((9,)),
             pltpu.VMEM((length + 8, width), F32),
-            pltpu.VMEM((16, width), BF16),
+            pltpu.VMEM((8, width), BF16),
             small,
             small,
             whole,
@@ -423,28 +513,7 @@
         compiler_params=pltpu.CompilerParams(
             vmem_limit_bytes=56 * 1024 * 1024, collective_id=0, has_side_effects=True
         ),
-    )(rows, params)
-    back = lax.all_to_all(
-        outs.reshape(n_head, tok_dev, outs.shape[1]),
-        "head",
-        split_axis=0,
-        concat_axis=0,
-        tiled=True,
-    )
-    grad_x = back[:, :, :width].transpose(1, 0, 2).reshape(tok_dev, n_head * width)
-
-    def gathered(at):
-        part = back[:, :, at : at + STATE].astype(F32) + back[
-            :, :, at + STATE : at + 2 * STATE
-        ].astype(F32)
-        part = part.reshape(GROUPS, per_group, tok_dev, STATE).sum(axis=1)
-        return part.transpose(1, 0, 2).reshape(tok_dev, GROUPS * STATE).astype(BF16)
-
-    at = width + 4 * STATE
-    g_dt = back[:, :, at : at + 3 * heads_dev].astype(F32)
-    g_dt = g_dt.reshape(n_head, tok_dev, 3, heads_dev).sum(axis=2)
-    grad_dt = g_dt.transpose(1, 0, 2).reshape(tok_dev, n_head * heads_dev)
-    return (grad_x, gathered(width), gathered(width + 2 * STATE), grad_dt)
+    )(x_in, grad_y, b_in, c_in, dt, params)
 
 
 def solution(mesh):

time: 115 us -> 96.1 us (0.84)
  the two profiles are of different devices: /device:TPU:8 before, /device:TPU:1 now
where the time goes in v3:
time: 96.1 us; the launch traced here: 95.8 us
  Pallas kernels  89.3 us (93%)
  local copies, waits for them, and re-layouts  5.73 us (6%)
    pallas_call x1, Pallas kernels, shards(): pl.pallas_call(functools.partial(block_kernel, n_ctx, n_head), out_shape=...  89.3 us
    unnamed x16, local copies, waits for them, and re-layouts  4.43 us

profile of v3, /device:TPU:1, one launch (start us, length us, event | category | flops | bytes accessed | tf_op | source)
XLA Modules:
  0.0 95.8 jit_solution(5437934087839568763)
XLA Ops:
  0.6 0.0 copy-start.4
  0.6 0.0 copy-start.5
  0.7 0.7 pad.7
  1.3 0.0 copy-done.5
  1.3 0.0 copy-start.2
  1.3 0.0 copy-done.4
  1.3 0.7 copy-done.2
  2.0 0.6 concatenate.3.par_ref
  2.6 89.3 %shard_map.120 = (bf16[8,16384]{1,0:T(8,128)(2,1)}, bf16[8,2048]{1,0:T(8,128)(2,1)}, bf16[8,2048]{1,0:T(8,128)(2,1)}, f32[8,256]{1,0:T(8,128)}) custom-call(bf16[8,16384]{1,0:T(8,128)(2,1)} %x_ref.1, bf16[8,16384]{1,0:T(8,128)(2,1)} %dy_ref.1, bf16[8,2048]{1,0:T(8,128)(2,1)} %b_ref.1, bf16[8,2048]{1,0:T(8,128)(2,1)} %c_ref.1, bf16[8,256]{1,0:T(8,128)(2,1)} %dt_ref.1, ...), custom_call_target="tpu_custom_call" | custom-call | tf_op jit(solution)/shard_map/pallas_call | solution.py:463
  92.0 0.0 copy-start.1
  92.0 1.7 %copy.17 = bf16[8,16384]{1,0:T(8,128)(2,1)} copy(bf16[8,16384]{1,0:T(8,128)(2,1)} %get-tuple-element.8) | data formatting | bytes 524288
  93.7 0.0 copy-done.1
  93.7 0.0 copy-start
  93.7 0.6 copy.18
  94.3 0.2 copy-done
  94.5 0.0 copy-start.3
  94.5 0.6 copy.19
  95.1 0.1 copy-done.3
  95.2 0.6 copy.20
  (1 shorter events, 0.0 us)
Async XLA Ops:
  0.6 0.7 copy-start.4
  0.6 0.7 copy-start.5
  1.3 0.7 copy-start.2
  92.0 1.7 %copy-start.1 = (bf16[8,2048]{1,0:T(8,128)(2,1)S(1)}, bf16[8,2048]{1,0:T(8,128)(2,1)}, u32[]{:S(2)}) copy-start(bf16[8,2048]{1,0:T(8,128)(2,1)} %get-tuple-element.9) | copy-start | bytes 98308
  93.7 0.8 copy-start
  94.5 0.7 copy-start.3

commit v4 on v3

v4 whole, which is shorter than its diff:
```python
import functools

import jax
import jax.numpy as jnp
from jax import lax
from jax.experimental import pallas as pl
from jax.experimental.pallas import tpu as pltpu
from jax.sharding import PartitionSpec as P

HEAD_DIM = 64
STATE = 256
GROUPS = 8
CONV = 4
LANES = 128
F32 = jnp.float32
BF16 = jnp.bfloat16
MESH = pl.DeviceIdType.MESH
PIECES = 4
CHUNK = 16 * PIECES


def nn(a, b):
    return lax.dot_general(a, b, (((1,), (0,)), ((), ())), preferred_element_type=F32)


def nt(a, b):
    return lax.dot_general(a, b, (((1,), (1,)), ((), ())), preferred_element_type=F32)


def split(value, pieces=2):
    parts = []
    for _ in range(pieces):
        part = value.astype(BF16)
        parts.append(part)
        value = value - part.astype(F32)
    return parts


def exact_by(dot, exact, wide):
    hi, lo = split(wide)
    return dot(exact, hi) + dot(exact, lo)


def wide_by(dot, wide, exact):
    hi, lo = split(wide)
    return dot(hi, exact) + dot(lo, exact)


def three(dot, left, right):
    lh, ll = split(left)
    rh, rl = split(right)
    return dot(lh, rh) + (dot(lh, rl) + dot(ll, rh))


def expand(cols, width, first=0):
    lane = lax.broadcasted_iota(jnp.int32, (cols.shape[0], LANES), 1)
    parts = [
        jnp.where(lane < HEAD_DIM, cols[:, h : h + 1], cols[:, h + 1 : h + 2])
        for h in range(first, first + width // HEAD_DIM, 2)
    ]
    return jnp.concatenate(parts, axis=1)


def segments(value, first=0):
    width = value.shape[1]
    row = lax.broadcasted_iota(jnp.int32, (width, LANES), 0)
    col = lax.broadcasted_iota(jnp.int32, (width, LANES), 1) - first
    pick = jnp.where(
        (row >= col * HEAD_DIM) & (row < (col + 1) * HEAD_DIM), 1.0, 0.0
    ).astype(BF16)
    return wide_by(nn, value, pick)


def triangle(length, lower):
    row = lax.broadcasted_iota(jnp.int32, (length, length), 0)
    col = lax.broadcasted_iota(jnp.int32, (length, length), 1)
    return row >= col if lower else row <= col


def convolve(x, par_ref, cols, ext):
    length = x.shape[0]
    ext[8 : 8 + length, :] = x
    conv = par_ref[4:5, cols] + par_ref[0:1, cols] * ext[5 : 5 + length, :]
    for k in range(1, CONV):
        conv = conv + par_ref[k : k + 1, cols] * ext[5 + k : 5 + k + length, :]
    return conv, 1.0 / (1.0 + jnp.exp(-conv))


def flat(ref):
    value = ref[...].astype(F32)
    return value.reshape(value.shape[0] * value.shape[1], value.shape[2])


def block_kernel(
    n_ctx,
    n_head,
    x_ref,
    dy_ref,
    b_ref,
    c_ref,
    dt_ref,
    par_ref,
    gx_ref,
    gb_ref,
    gc_ref,
    gdt_ref,
    x_buf,
    dy_buf,
    b_buf,
    c_buf,
    dt_buf,
    gx_buf,
    gb_buf,
    gc_buf,
    gdt_buf,
    gb_all,
    gc_all,
    gdt_all,
    head_send,
    head_recv,
    ext,
    edge,
    top_out,
    top_in,
    mine,
    other,
    sib_local,
    decay_own,
    decay_sib,
    chain_in,
    chain_out,
    sib_out,
    sib_in,
    gram_sum,
    cumul_sum,
    inner,
    edge_sems,
    top_sems,
    local_sems,
    decay_sems,
    chain_send,
    chain_recv,
    sib_send,
    sib_recv,
):
    pieces, length, part = ext.shape[0], ext.shape[1] - 8, ext.shape[2]
    width = pieces * part
    tok_dev = x_ref.shape[0]
    heads_dev = width // HEAD_DIM
    per_group = n_head // GROUPS
    per_tile = LANES // heads_dev
    head = lax.axis_index("head")
    me = lax.axis_index("ctx")
    core = lax.rem(me, 2)
    chip = lax.div(me, 2)
    chips = n_ctx // 2
    sign = 1 - 2 * core
    place = core * (chips - 1) + sign * chip
    sibling = me + sign
    per_piece = part // HEAD_DIM
    chunks = STATE // CHUNK
    pace = max(chips // pieces, 1)
    lag = lax.div(place + pace - 1, pace)
    late = place >= max(chips // 2 - 1, 1)
    early = jnp.logical_not(late)
    ahead = lax.rem(me + 2 * sign + n_ctx, n_ctx)
    following = lax.rem(me + 1, n_ctx)
    leading = lax.rem(me + n_ctx - 1, n_ctx)

    def remote(src, dst, sems, device, axis="ctx"):
        return pltpu.make_async_remote_copy(
            src_ref=src,
            dst_ref=dst,
            send_sem=sems[0],
            recv_sem=sems[1],
            device_id={axis: device},
            device_id_type=MESH,
        )

    barrier = pltpu.get_barrier_semaphore()
    for by in (1, 2, n_ctx - 2, n_ctx - 1):
        pl.semaphore_signal(
            barrier,
            inc=1,
            device_id={"ctx": lax.rem(me + by, n_ctx)},
            device_id_type=MESH,
        )

    def greet(k, _):
        pl.semaphore_signal(
            barrier,
            inc=1,
            device_id={"head": lax.rem(head + k, n_head)},
            device_id_type=MESH,
        )
        return 0

    lax.fori_loop(1, n_head, greet, 0)
    pl.semaphore_wait(barrier, 3 + n_head)

    def scatter(kind, source, target):
        def step(k, _):
            to = lax.rem(head + k, n_head)
            remote(
                source(to), target, (head_send.at[kind], head_recv.at[kind]), to, "head"
            ).start()
            return 0

        lax.fori_loop(1, n_head, step, 0)
        pltpu.make_async_copy(source(head), target, head_recv.at[kind]).start()

    def arrived(kind, buffer):
        pltpu.make_async_copy(buffer, buffer, head_recv.at[kind]).wait()

    def sent(kind, buffer):
        pltpu.make_async_copy(buffer, buffer, head_send.at[kind]).wait()

    def lanes(ref, start, size):
        return ref.at[:, pl.ds(pl.multiple_of(start, LANES), size)]

    def send_piece(kind, ref, buffer, p):
        scatter(
            kind + p,
            lambda to: lanes(ref, to * width + p * part, part),
            buffer.at[p, head],
        )

    x_kind, dy_kind, out_kind = 3, 3 + pieces, 3 + 2 * pieces
    scatter(2, lambda to: lanes(dt_ref, lax.div(to, per_tile) * LANES, LANES), dt_buf.at[head])
    scatter(0, lambda to: lanes(b_ref, lax.div(to, per_group) * STATE, STATE), b_buf.at[head])
    scatter(1, lambda to: lanes(c_ref, lax.div(to, per_group) * STATE, STATE), c_buf.at[head])
    send_piece(x_kind, x_ref, x_buf, 0)
    for p in range(pieces):
        if p + 1 < pieces:
            send_piece(x_kind, x_ref, x_buf, p + 1)
        send_piece(dy_kind, dy_ref, dy_buf, p)

    @pl.when(place == 0)
    def _():
        chain_in[...] = jnp.zeros_like(chain_in)

    def edge_copy(p):
        return remote(
            x_buf.at[p, n_head - 1, tok_dev - 8 : tok_dev, :],
            edge.at[p],
            (edge_sems.at[0, p], edge_sems.at[1, p]),
            following,
        )

    def local_copy(p):
        return remote(
            other.at[p], sib_local.at[p], (local_sems.at[0, p], local_sems.at[1, p]), sibling
        )

    def top_copy(p):
        return remote(
            top_out.at[p], top_in.at[p], (top_sems.at[0, p], top_sems.at[1, p]), leading
        )

    def chain_copy(p, c):
        rows = pl.ds(pl.multiple_of(c * CHUNK, CHUNK), CHUNK)
        return remote(
            chain_out.at[p, rows, :],
            chain_in.at[p, rows, :],
            (chain_send.at[p, c], chain_recv.at[p, c]),
            ahead,
        )

    def sib_copy(p, c):
        rows = pl.ds(pl.multiple_of(c * CHUNK, CHUNK), CHUNK)
        return remote(
            sib_out.at[p, rows, :],
            sib_in.at[p, rows, :],
            (sib_send.at[p, c], sib_recv.at[p, c]),
            sibling,
        )

    lower = triangle(length, True)
    upper = triangle(length, False)
    lane = lax.broadcasted_iota(jnp.int32, (length, LANES), 1)
    arrived(2, dt_buf)
    shift = lax.rem(LANES - lax.rem(head, per_tile) * heads_dev, LANES)
    dt = jnp.where(lane < heads_dev, pltpu.roll(flat(dt_buf), shift, 1), 0.0)
    rate = par_ref[6:7, 0:LANES]
    cumul = -rate * nn(jnp.where(lower, 1.0, 0.0).astype(BF16), dt.astype(BF16))
    grow_cols = jnp.exp(cumul)
    tail_cols = jnp.exp(cumul[length - 1 : length, :] - cumul)
    for p in range(pieces):
        last = expand(grow_cols[length - 8 : length, :], part, p * per_piece)
        decay_own[p] = jnp.broadcast_to(last[7:8, :], (8, part))
    decay_copy = remote(
        decay_own, decay_sib, (decay_sems.at[0], decay_sems.at[1]), sibling
    )
    decay_copy.start()
    arrived(0, b_buf)
    arrived(1, c_buf)
    b32 = flat(b_buf)
    c32 = flat(c_buf)
    b16 = b32.astype(BF16)
    c16 = c32.astype(BF16)
    b_turned = b32.T.astype(BF16)
    c_turned = c32.T.astype(BF16)
    turned = cumul.T
    gram = nt(c16, b16)
    gram_turned = nt(b16, c16)
    gram_sum[...] = jnp.zeros_like(gram_sum)
    cumul_sum[...] = jnp.zeros_like(cumul_sum)
    first_core = core == 0

    def local(p):
        if p == 0:
            arrived(x_kind, x_buf.at[0])
            edge_copy(0).start()
        if p + 1 < pieces:
            arrived(x_kind + p + 1, x_buf.at[p + 1])
            edge_copy(p + 1).start()
        arrived(dy_kind + p, dy_buf.at[p])
        cols = slice(p * part, (p + 1) * part)
        dy = flat(dy_buf.at[p])
        grow = expand(grow_cols, part, p * per_piece)
        tail = expand(tail_cols, part, p * per_piece)
        dt_wide = expand(dt, part, p * per_piece)
        dy_grown = dy * grow
        pull = exact_by(nn, c_turned, dy_grown)
        edge_copy(p).wait()
        ext[p, 0:8, :] = jnp.where(me > 0, edge[p].astype(F32), 0.0)
        conv, sig = convolve(flat(x_buf.at[p]), par_ref, cols, ext.at[p])
        activ = conv * sig
        slope = sig * (1.0 + conv * (1.0 - sig))
        source = activ * dt_wide
        state = exact_by(nn, b_turned, source * tail)
        other[p] = jnp.where(first_core, pull, state)
        local_copy(p).start()
        mine[p] = jnp.where(first_core, state, pull)
        return (cols, dy, grow, tail, dt_wide, dy_grown, activ, slope, source)

    def chain(p):
        local_copy(p).wait_recv()

        def hop(c, _):
            rows = pl.ds(pl.multiple_of(c * CHUNK, CHUNK), CHUNK)

            @pl.when(place > 0)
            def _():
                chain_copy(p, c).wait_recv()

            here = decay_own[p, 0:1, :] * chain_in[p, rows, :] + mine[p, rows, :]
            chain_out[p, rows, :] = decay_sib[p, 0:1, :] * here + sib_local[p, rows, :]

            @pl.when(place < chips - 1)
            def _():
                chain_copy(p, c).start()

            sib_out[p, rows, :] = here
            sib_copy(p, c).start()
            return 0

        lax.fori_loop(0, chunks, hop, 0)

    def within(p):
        dy, source = held[p][1], held[p][8]
        g_gram = gram_sum[...]
        g_cumul = cumul_sum[...]
        for pair in range(part // LANES):
            at = slice(pair * LANES, (pair + 1) * LANES)
            src_hi, src_lo = split(source[:, at])
            dy16 = dy[:, at].astype(BF16)
            halves = []
            for side in range(2):
                h = p * per_piece + 2 * pair + side
                own = lane < HEAD_DIM if side == 0 else lane >= HEAD_DIM
                dy_own = jnp.where(own, dy[:, at], 0.0).astype(BF16)
                col = cumul[:, h : h + 1]
                row = turned[h : h + 1, :]
                decay = jnp.where(lower, jnp.exp(jnp.minimum(col - row, 0.0)), 0.0)
                inside = decay * (nt(dy_own, src_hi) + nt(dy_own, src_lo))
                g_gram = g_gram + inside
                g_cumul = g_cumul + jnp.where(
                    lane == h, jnp.sum(inside * gram, axis=1, keepdims=True), 0.0
                )
                mixing = gram_turned * jnp.where(
                    upper, jnp.exp(jnp.minimum(row - col, 0.0)), 0.0
                )
                halves.append(wide_by(nn, mixing, dy16))
            inner[p, :, at] = jnp.where(lane < HEAD_DIM, halves[0], halves[1])
        gram_sum[...] = g_gram
        cumul_sum[...] = g_cumul

    held = []
    for step in range(pieces):
        held.append(local(step))
        if step == 0:
            decay_copy.wait()

        @pl.when(step >= lag)
        def _():
            chain(step - lag)

        if step + 1 < pieces:
            within(step)

    @pl.when(late)
    def _():
        within(pieces - 1)

    for j in range(1, pieces):

        @pl.when(early & (lag >= j))
        def _():
            chain(pieces - 1 - lag + j)

    @pl.when(early)
    def _():
        within(pieces - 1)

    def by_token(value):
        return value.reshape(n_head, tok_dev, value.shape[1])

    def finish(p):
        cols = held[p][0]
        top_copy(p).wait()
        ext[p, length : length + 8, :] = jnp.where(me < n_ctx - 1, top_in[p], 0.0)
        g_x = par_ref[3:4, cols] * ext[p, 0:length, :]
        for k in range(CONV - 1):
            back = CONV - 1 - k
            g_x = g_x + par_ref[k : k + 1, cols] * ext[p, back : back + length, :]
        gx_buf[p] = by_token(g_x).astype(BF16)
        scatter(
            out_kind + 3,
            lambda to: gx_buf.at[p, to],
            lanes(gx_ref, head * width + p * part, part),
        )

    g_gram = gram_sum[...]
    g_b = wide_by(nn, g_gram.T, c16)
    g_c = wide_by(nn, g_gram, b16)
    direct = jnp.zeros((length, LANES), F32)
    g_cumul = cumul_sum[...]
    total = jnp.zeros((16, LANES), F32)
    for p in range(pieces):

        @pl.when(late & (lag > pieces - 1 - p))
        def _():
            chain(p)

        lax.fori_loop(0, chunks, lambda c, _: (sib_copy(p, c).wait_recv(), 0)[1], 0)
        cols, dy, grow, tail, dt_wide, dy_grown, activ, slope, source = held[p]
        state = jnp.where(first_core, chain_in[p], sib_in[p])
        pull = jnp.where(first_core, sib_in[p], chain_in[p])
        pulled = tail * exact_by(nn, b16, pull)
        g_source = inner[p] + pulled
        skip = expand(par_ref[7:8, 0:LANES], part, p * per_piece)
        g_conv = (dt_wide * g_source + skip * dy) * slope
        ext[p, 0:length, :] = g_conv
        top_out[p] = g_conv[0:8, :]
        top_copy(p).start()
        g_b = g_b + three(nt, source * tail, pull)
        g_c = g_c + three(nt, dy_grown, state)
        if p + 1 == pieces:
            gb_buf[...] = by_token(g_b)
            scatter(out_kind, lambda to: gb_buf.at[to], gb_all.at[head])
            gc_buf[...] = by_token(g_c)
            scatter(out_kind + 1, lambda to: gc_buf.at[to], gc_all.at[head])
        first = p * per_piece
        direct = direct + segments(activ * g_source, first)
        g_cumul = g_cumul + segments(dy_grown * exact_by(nn, c16, state), first)
        carried = jnp.sum(source * pulled, axis=0, keepdims=True) + grow[
            length - 1 : length, :
        ] * jnp.sum(state * pull, axis=0, keepdims=True)
        total = total + segments(jnp.broadcast_to(carried, (16, part)), first)
        if p > 0:
            finish(p - 1)
    finish(pieces - 1)

    after = jnp.where(upper, 1.0, 0.0).astype(BF16)
    terms = split(g_cumul - dt * direct, 3)
    later = nn(after, terms[0]) + (nn(after, terms[1]) + nn(after, terms[2]))
    g_dt = direct - rate * (later + total[0:1, :])
    merged = jnp.zeros((length, LANES), F32)
    for j, term in enumerate(split(g_dt, 3)):
        term = term.astype(F32)
        merged = merged + (pltpu.roll(term, j * heads_dev, 1) if j else term)
    gdt_buf[...] = by_token(merged).astype(BF16)
    scatter(out_kind + 2, lambda to: gdt_buf.at[to], gdt_all.at[head])

    for kind, buffer, result in ((out_kind, gb_all, gb_ref), (out_kind + 1, gc_all, gc_ref)):
        arrived(kind, buffer)
        for g in range(GROUPS):
            summed = buffer[g * per_group]
            for j in range(1, per_group):
                summed = summed + buffer[g * per_group + j]
            result[:, g * STATE : (g + 1) * STATE] = summed.astype(BF16)
    arrived(out_kind + 2, gdt_all)
    own = lax.broadcasted_iota(jnp.int32, (tok_dev, LANES), 1) < heads_dev
    for tile in range(n_head // per_tile):
        summed = jnp.zeros((tok_dev, LANES), F32)
        for j in range(per_tile):
            value = gdt_all[tile * per_tile + j].astype(F32)
            value = (
                value
                + pltpu.roll(value, LANES - heads_dev, 1)
                + pltpu.roll(value, LANES - 2 * heads_dev, 1)
            )
            value = jnp.where(own, value, 0.0)
            summed = summed + (pltpu.roll(value, j * heads_dev, 1) if j else value)
        gdt_ref[:, tile * LANES : (tile + 1) * LANES] = summed
    arrived(out_kind + 3, gx_ref)

    for kind, buffer in enumerate((b_buf, c_buf, dt_buf)):
        sent(kind, buffer.at[0 : n_head - 1])
    for p in range(pieces):
        sent(x_kind + p, x_buf.at[p, 0 : n_head - 1])
        sent(dy_kind + p, dy_buf.at[p, 0 : n_head - 1])
        local_copy(p).wait_send()

        def drain(c, _):
            @pl.when(place < chips - 1)
            def _():
                chain_copy(p, c).wait_send()

            sib_copy(p, c).wait_send()
            return 0

        lax.fori_loop(0, chunks, drain, 0)
    for kind, buffer in enumerate((gb_buf, gc_buf, gdt_buf)):
        sent(out_kind + kind, buffer.at[0 : n_head - 1])
    sent(out_kind + 3, gx_buf.at[:, 0 : n_head - 1])


def shards(x_in, grad_y, b_in, c_in, dt, conv_weight, conv_bias, decay_rate, skip):
    n_head = lax.axis_size("head")
    n_ctx = lax.axis_size("ctx")
    per_group = n_head // GROUPS
    tok_dev = x_in.shape[0]
    heads_dev = decay_rate.shape[0]
    width = heads_dev * HEAD_DIM
    length = tok_dev * n_head

    wide = lambda value: jnp.pad(value[None, :], ((0, 0), (0, width - heads_dev)))
    params = jnp.concatenate(
        [conv_weight, conv_bias[None, :], conv_bias[None, :], wide(decay_rate), wide(skip)], axis=0
    )
    part = width // PIECES
    held = lambda size, kind: pltpu.VMEM((n_head, tok_dev, size), kind)
    cut = lambda kind: pltpu.VMEM((PIECES, n_head, tok_dev, part), kind)
    small = lambda kind: pltpu.VMEM((PIECES, 8, part), kind)
    whole = pltpu.VMEM((PIECES, STATE, part), F32)
    dma = pltpu.SemaphoreType.DMA
    many = dma((PIECES, STATE // CHUNK))
    return pl.pallas_call(
        functools.partial(block_kernel, n_ctx, n_head),
        out_shape=(
            jax.ShapeDtypeStruct(x_in.shape, BF16),
            jax.ShapeDtypeStruct(b_in.shape, BF16),
            jax.ShapeDtypeStruct(c_in.shape, BF16),
            jax.ShapeDtypeStruct(dt.shape, F32),
        ),
        in_specs=[pl.BlockSpec(memory_space=pltpu.VMEM)] * 6,
        out_specs=[pl.BlockSpec(memory_space=pltpu.VMEM)] * 4,
        scratch_shapes=[
            cut(BF16),
            cut(BF16),
            held(STATE, BF16),
            held(STATE, BF16),
            held(LANES, BF16),
            cut(BF16),
            held(STATE, F32),
            held(STATE, F32),
            held(LANES, BF16),
            held(STATE, F32),
            held(STATE, F32),
            held(LANES, BF16),
            dma((7 + 2 * PIECES,)),
            dma((7 + 2 * PIECES,)),
            pltpu.VMEM((PIECES, length + 8, part), F32),
            small(BF16),
            small(F32),
            small(F32),
            whole,
            whole,
            whole,
            small(F32),
            small(F32),
            whole,
            whole,
            whole,
            whole,
            pltpu.VMEM((length, length), F32),
            pltpu.VMEM((length, LANES), F32),
            pltpu.VMEM((PIECES, length, part), F32),
            dma((2, PIECES)),
            dma((2, PIECES)),
            dma((2, PIECES)),
            dma((2,)),
            many,
            many,
            many,
            many,
        ],
        compiler_params=pltpu.CompilerParams(
            vmem_limit_bytes=56 * 1024 * 1024, collective_id=0, has_side_effects=True
        ),
    )(x_in, grad_y, b_in, c_in, dt, params)


def solution(mesh):
    token = P(("ctx", "head"), None)
    in_specs = (token,) * 5 + (P(None, "head"), P("head"), P("head"), P("head"))
    return jax.shard_map(
        shards, mesh=mesh, in_specs=in_specs, out_specs=(token,) * 4, check_vma=False
    )
```

time: 96.1 us -> 98 us (1.020)
  Pallas kernels: 89.3 us -> 91.2 us
    pallas_call x1, Pallas kernels: 89.3 us -> 91.2 us  [shards(): pl.pallas_call(functools.partial(block_kernel, n_ctx, n_head), out_shape=...]
where the time goes in v4:
time: 98 us; the launch traced here: 97.7 us
  Pallas kernels  91.2 us (93%)
  local copies, waits for them, and re-layouts  5.73 us (6%)
    pallas_call x1, Pallas kernels, shards(): pl.pallas_call(functools.partial(block_kernel, n_ctx, n_head), out_shape=...  91.2 us
    unnamed x16, local copies, waits for them, and re-layouts  4.43 us

profile of v4, /device:TPU:1, one launch (start us, length us, event | category | flops | bytes accessed | tf_op | source)
XLA Modules:
  0.0 97.7 jit_solution(16546760923532485719)
XLA Ops:
  0.6 0.0 copy-start.4
  0.6 0.0 copy-start.5
  0.7 0.7 pad.7
  1.3 0.0 copy-done.5
  1.3 0.0 copy-start.2
  1.3 0.0 copy-done.4
  1.3 0.7 copy-done.2
  2.0 0.6 concatenate.3.par_ref
  2.6 91.2 %shard_map.120 = (bf16[8,16384]{1,0:T(8,128)(2,1)}, bf16[8,2048]{1,0:T(8,128)(2,1)}, bf16[8,2048]{1,0:T(8,128)(2,1)}, f32[8,256]{1,0:T(8,128)}) custom-call(bf16[8,16384]{1,0:T(8,128)(2,1)} %x_ref.1, bf16[8,16384]{1,0:T(8,128)(2,1)} %dy_ref.1, bf16[8,2048]{1,0:T(8,128)(2,1)} %b_ref.1, bf16[8,2048]{1,0:T(8,128)(2,1)} %c_ref.1, bf16[8,256]{1,0:T(8,128)(2,1)} %dt_ref.1, ...), custom_call_target="tpu_custom_call" | custom-call | tf_op jit(solution)/shard_map/pallas_call | solution.py:550
  93.9 0.0 copy-start.1
  93.9 1.7 %copy.17 = bf16[8,16384]{1,0:T(8,128)(2,1)} copy(bf16[8,16384]{1,0:T(8,128)(2,1)} %get-tuple-element.8) | data formatting | bytes 524288
  95.6 0.0 copy-done.1
  95.6 0.0 copy-start
  95.6 0.6 copy.18
  96.2 0.2 copy-done
  96.3 0.0 copy-start.3
  96.3 0.6 copy.19
  97.0 0.1 copy-done.3
  97.1 0.6 copy.20
  (1 shorter events, 0.0 us)
Async XLA Ops:
  0.6 0.7 copy-start.4
  0.6 0.7 copy-start.5
  1.3 0.7 copy-start.2
  93.9 1.7 %copy-start.1 = (bf16[8,2048]{1,0:T(8,128)(2,1)S(1)}, bf16[8,2048]{1,0:T(8,128)(2,1)}, u32[]{:S(2)}) copy-start(bf16[8,2048]{1,0:T(8,128)(2,1)} %get-tuple-element.9) | copy-start | bytes 98308
  95.6 0.8 copy-start
  96.3 0.7 copy-start.3

commit v5 on v4

--- a/solution.py
+++ b/solution.py
@@ -15,7 +15,7 @@
 F32 = jnp.float32
 BF16 = jnp.bfloat16
 MESH = pl.DeviceIdType.MESH
-PIECES = 4
+PIECES = 2
 CHUNK = 16 * PIECES
 
 
@@ -86,8 +86,25 @@
     return conv, 1.0 / (1.0 + jnp.exp(-conv))
 
 
-def flat(ref):
-    value = ref[...].astype(F32)
+def layout(pieces, part):
+    boxes = [["dt", "b", "c", "x0"]] + [[] for _ in range(pieces - 1)]
+    for p in range(pieces):
+        if p + 1 < pieces:
+            boxes[p].append("x%d" % (p + 1))
+        boxes[p].append("dy%d" % p)
+    sizes, plan = [], {}
+    for box, names in enumerate(boxes):
+        start = 0
+        for name in names:
+            size = {"dt": LANES, "b": STATE, "c": STATE}.get(name, part)
+            plan[name] = (box, start, size, int(name[-1]) if name[-1].isdigit() else 0)
+            start += size
+        sizes.append(start)
+    return sizes, plan
+
+
+def flat(value):
+    value = value.astype(F32)
     return value.reshape(value.shape[0] * value.shape[1], value.shape[2])
 
 
@@ -104,17 +121,12 @@
     gb_ref,
     gc_ref,
     gdt_ref,
-    x_buf,
-    dy_buf,
-    b_buf,
-    c_buf,
-    dt_buf,
+    stage,
+    got,
     gx_buf,
-    gb_buf,
-    gc_buf,
+    gp_buf,
     gdt_buf,
-    gb_all,
-    gc_all,
+    gp_all,
     gdt_all,
     head_send,
     head_recv,
@@ -177,6 +189,21 @@
             device_id_type=MESH,
         )
 
+    plan = layout(pieces, part)[1]
+    for to in range(n_head):
+        for name, (box, start, size, p) in plan.items():
+            if name == "dt":
+                ref, first = dt_ref, to // per_tile * LANES
+            elif name in ("b", "c"):
+                ref, first = (b_ref if name == "b" else c_ref), to // per_group * STATE
+            else:
+                ref, first = (x_ref if name[0] == "x" else dy_ref), to * width + p * part
+            stage[box][to, :, start : start + size] = ref[:, first : first + size]
+
+    def piece_of(name):
+        box, start, size, _ = plan[name]
+        return flat(got[box][:, :, start : start + size])
+
     barrier = pltpu.get_barrier_semaphore()
     for by in (1, 2, n_ctx - 2, n_ctx - 1):
         pl.semaphore_signal(
@@ -218,30 +245,18 @@
     def lanes(ref, start, size):
         return ref.at[:, pl.ds(pl.multiple_of(start, LANES), size)]
 
-    def send_piece(kind, ref, buffer, p):
-        scatter(
-            kind + p,
-            lambda to: lanes(ref, to * width + p * part, part),
-            buffer.at[p, head],
-        )
-
-    x_kind, dy_kind, out_kind = 3, 3 + pieces, 3 + 2 * pieces
-    scatter(2, lambda to: lanes(dt_ref, lax.div(to, per_tile) * LANES, LANES), dt_buf.at[head])
-    scatter(0, lambda to: lanes(b_ref, lax.div(to, per_group) * STATE, STATE), b_buf.at[head])
-    scatter(1, lambda to: lanes(c_ref, lax.div(to, per_group) * STATE, STATE), c_buf.at[head])
-    send_piece(x_kind, x_ref, x_buf, 0)
+    out_kind = pieces
     for p in range(pieces):
-        if p + 1 < pieces:
-            send_piece(x_kind, x_ref, x_buf, p + 1)
-        send_piece(dy_kind, dy_ref, dy_buf, p)
+        scatter(p, lambda to: stage[p].at[to], got[p].at[head])
 
     @pl.when(place == 0)
     def _():
         chain_in[...] = jnp.zeros_like(chain_in)
 
     def edge_copy(p):
+        box, start, size, _ = plan["x%d" % p]
         return remote(
-            x_buf.at[p, n_head - 1, tok_dev - 8 : tok_dev, :],
+            got[box].at[n_head - 1, tok_dev - 8 : tok_dev, start : start + size],
             edge.at[p],
             (edge_sems.at[0, p], edge_sems.at[1, p]),
             following,
@@ -278,9 +293,12 @@
     lower = triangle(length, True)
     upper = triangle(length, False)
     lane = lax.broadcasted_iota(jnp.int32, (length, LANES), 1)
-    arrived(2, dt_buf)
+    arrived(0, got[0])
+    edge_copy(0).start()
+    if pieces > 1:
+        edge_copy(1).start()
     shift = lax.rem(LANES - lax.rem(head, per_tile) * heads_dev, LANES)
-    dt = jnp.where(lane < heads_dev, pltpu.roll(flat(dt_buf), shift, 1), 0.0)
+    dt = jnp.where(lane < heads_dev, pltpu.roll(piece_of("dt"), shift, 1), 0.0)
     rate = par_ref[6:7, 0:LANES]
     cumul = -rate * nn(jnp.where(lower, 1.0, 0.0).astype(BF16), dt.astype(BF16))
     grow_cols = jnp.exp(cumul)
@@ -292,10 +310,8 @@
         decay_own, decay_sib, (decay_sems.at[0], decay_sems.at[1]), sibling
     )
     decay_copy.start()
-    arrived(0, b_buf)
-    arrived(1, c_buf)
-    b32 = flat(b_buf)
-    c32 = flat(c_buf)
+    b32 = piece_of("b")
+    c32 = piece_of("c")
     b16 = b32.astype(BF16)
     c16 = c32.astype(BF16)
     b_turned = b32.T.astype(BF16)
@@ -308,15 +324,12 @@
     first_core = core == 0
 
     def local(p):
-        if p == 0:
-            arrived(x_kind, x_buf.at[0])
-            edge_copy(0).start()
-        if p + 1 < pieces:
-            arrived(x_kind + p + 1, x_buf.at[p + 1])
+        if p > 0:
+            arrived(p, got[p])
+        if 0 < p < pieces - 1:
             edge_copy(p + 1).start()
-        arrived(dy_kind + p, dy_buf.at[p])
         cols = slice(p * part, (p + 1) * part)
-        dy = flat(dy_buf.at[p])
+        dy = piece_of("dy%d" % p)
         grow = expand(grow_cols, part, p * per_piece)
         tail = expand(tail_cols, part, p * per_piece)
         dt_wide = expand(dt, part, p * per_piece)
@@ -324,7 +337,7 @@
         pull = exact_by(nn, c_turned, dy_grown)
         edge_copy(p).wait()
         ext[p, 0:8, :] = jnp.where(me > 0, edge[p].astype(F32), 0.0)
-        conv, sig = convolve(flat(x_buf.at[p]), par_ref, cols, ext.at[p])
+        conv, sig = convolve(piece_of("x%d" % p), par_ref, cols, ext.at[p])
         activ = conv * sig
         slope = sig * (1.0 + conv * (1.0 - sig))
         source = activ * dt_wide
@@ -426,7 +439,7 @@
             g_x = g_x + par_ref[k : k + 1, cols] * ext[p, back : back + length, :]
         gx_buf[p] = by_token(g_x).astype(BF16)
         scatter(
-            out_kind + 3,
+            out_kind + 2,
             lambda to: gx_buf.at[p, to],
             lanes(gx_ref, head * width + p * part, part),
         )
@@ -457,10 +470,9 @@
         g_b = g_b + three(nt, source * tail, pull)
         g_c = g_c + three(nt, dy_grown, state)
         if p + 1 == pieces:
-            gb_buf[...] = by_token(g_b)
-            scatter(out_kind, lambda to: gb_buf.at[to], gb_all.at[head])
-            gc_buf[...] = by_token(g_c)
-            scatter(out_kind + 1, lambda to: gc_buf.at[to], gc_all.at[head])
+            gp_buf[:, :, 0:STATE] = by_token(g_b)
+            gp_buf[:, :, STATE : 2 * STATE] = by_token(g_c)
+            scatter(out_kind, lambda to: gp_buf.at[to], gp_all.at[head])
         first = p * per_piece
         direct = direct + segments(activ * g_source, first)
         g_cumul = g_cumul + segments(dy_grown * exact_by(nn, c16, state), first)
@@ -481,16 +493,17 @@
         term = term.astype(F32)
         merged = merged + (pltpu.roll(term, j * heads_dev, 1) if j else term)
     gdt_buf[...] = by_token(merged).astype(BF16)
-    scatter(out_kind + 2, lambda to: gdt_buf.at[to], gdt_all.at[head])
-
-    for kind, buffer, result in ((out_kind, gb_all, gb_ref), (out_kind + 1, gc_all, gc_ref)):
-        arrived(kind, buffer)
-        for g in range(GROUPS):
-            summed = buffer[g * per_group]
-            for j in range(1, per_group):
-                summed = summed + buffer[g * per_group + j]
-            result[:, g * STATE : (g + 1) * STATE] = summed.astype(BF16)
-    arrived(out_kind + 2, gdt_all)
+    scatter(out_kind + 1, lambda to: gdt_buf.at[to], gdt_all.at[head])
+
+    arrived(out_kind, gp_all)
+    for g in range(GROUPS):
+        summed = gp_all[g * per_group]
+        for j in range(1, per_group):
+            summed = summed + gp_all[g * per_group + j]
+        summed = summed.astype(BF16)
+        gb_ref[:, g * STATE : (g + 1) * STATE] = summed[:, 0:STATE]
+        gc_ref[:, g * STATE : (g + 1) * STATE] = summed[:, STATE : 2 * STATE]
+    arrived(out_kind + 1, gdt_all)
     own = lax.broadcasted_iota(jnp.int32, (tok_dev, LANES), 1) < heads_dev
     for tile in range(n_head // per_tile):
         summed = jnp.zeros((tok_dev, LANES), F32)
@@ -504,13 +517,10 @@
             value = jnp.where(own, value, 0.0)
             summed = summed + (pltpu.roll(value, j * heads_dev, 1) if j else value)
         gdt_ref[:, tile * LANES : (tile + 1) * LANES] = summed
-    arrived(out_kind + 3, gx_ref)
-
-    for kind, buffer in enumerate((b_buf, c_buf, dt_buf)):
-        sent(kind, buffer.at[0 : n_head - 1])
+    arrived(out_kind + 2, gx_ref)
+
     for p in range(pieces):
-        sent(x_kind + p, x_buf.at[p, 0 : n_head - 1])
-        sent(dy_kind + p, dy_buf.at[p, 0 : n_head - 1])
+        sent(p, stage[p].at[0 : n_head - 1])
         local_copy(p).wait_send()
 
         def drain(c, _):
@@ -522,9 +532,9 @@
             return 0
 
         lax.fori_loop(0, chunks, drain, 0)
-    for kind, buffer in enumerate((gb_buf, gc_buf, gdt_buf)):
-        sent(out_kind + kind, buffer.at[0 : n_head - 1])
-    sent(out_kind + 3, gx_buf.at[:, 0 : n_head - 1])
+    sent(out_kind, gp_buf.at[0 : n_head - 1])
+    sent(out_kind + 1, gdt_buf.at[0 : n_head - 1])
+    sent(out_kind + 2, gx_buf.at[:, 0 : n_head - 1])
 
 
 def shards(x_in, grad_y, b_in, c_in, dt, conv_weight, conv_bias, decay_rate, skip):
@@ -541,6 +551,7 @@
         [conv_weight, conv_bias[None, :], conv_bias[None, :], wide(decay_rate), wide(skip)], axis=0
     )
     part = width // PIECES
+    sizes = layout(PIECES, part)[0]
     held = lambda size, kind: pltpu.VMEM((n_head, tok_dev, size), kind)
     cut = lambda kind: pltpu.VMEM((PIECES, n_head, tok_dev, part), kind)
     small = lambda kind: pltpu.VMEM((PIECES, 8, part), kind)
@@ -558,20 +569,15 @@
         in_specs=[pl.BlockSpec(memory_space=pltpu.VMEM)] * 6,
         out_specs=[pl.BlockSpec(memory_space=pltpu.VMEM)] * 4,
         scratch_shapes=[
+            [held(size, BF16) for size in sizes],
+            [held(size, BF16) for size in sizes],
             cut(BF16),
-            cut(BF16),
-            held(STATE, BF16),
-            held(STATE, BF16),
+            held(2 * STATE, F32),
             held(LANES, BF16),
-            cut(BF16),
-            held(STATE, F32),
-            held(STATE, F32),
+            held(2 * STATE, F32),
             held(LANES, BF16),
-            held(STATE, F32),
-            held(STATE, F32),
-            held(LANES, BF16),
-            dma((7 + 2 * PIECES,)),
-            dma((7 + 2 * PIECES,)),
+            dma((3 + PIECES,)),
+            dma((3 + PIECES,)),
             pltpu.VMEM((PIECES, length + 8, part), F32),
             small(BF16),
             small(F32),

time: 98 us -> 98 us (level); the launches traced: 97.7 us -> 96.5 us
  Pallas kernels: 91.2 us -> 90.1 us
    pallas_call x1, Pallas kernels: 91.2 us -> 90.1 us  [shards(): pl.pallas_call(functools.partial(block_kernel, n_ctx, n_head), out_shape=...]
where the time goes in v5:
time: 98 us; the launch traced here: 96.5 us
  Pallas kernels  90.1 us (92%)
  local copies, waits for them, and re-layouts  5.73 us (6%)
    pallas_call x1, Pallas kernels, shards(): pl.pallas_call(functools.partial(block_kernel, n_ctx, n_head), out_shape=...  90.1 us
    unnamed x16, local copies, waits for them, and re-layouts  4.43 us

profile of v5, /device:TPU:1, one launch (start us, length us, event | category | flops | bytes accessed | tf_op | source)
XLA Modules:
  0.0 96.5 jit_solution(3865940261358315567)
XLA Ops:
  0.6 0.0 copy-start.4
  0.6 0.0 copy-start.5
  0.7 0.7 pad.7
  1.3 0.0 copy-done.5
  1.3 0.0 copy-start.2
  1.3 0.0 copy-done.4
  1.3 0.7 copy-done.2
  2.0 0.6 concatenate.3.par_ref
  2.6 90.1 %shard_map.120 = (bf16[8,16384]{1,0:T(8,128)(2,1)}, bf16[8,2048]{1,0:T(8,128)(2,1)}, bf16[8,2048]{1,0:T(8,128)(2,1)}, f32[8,256]{1,0:T(8,128)}) custom-call(bf16[8,16384]{1,0:T(8,128)(2,1)} %x_ref.1, bf16[8,16384]{1,0:T(8,128)(2,1)} %dy_ref.1, bf16[8,2048]{1,0:T(8,128)(2,1)} %b_ref.1, bf16[8,2048]{1,0:T(8,128)(2,1)} %c_ref.1, bf16[8,256]{1,0:T(8,128)(2,1)} %dt_ref.1, ...), custom_call_target="tpu_custom_call" | custom-call | tf_op jit(solution)/shard_map/pallas_call | solution.py:561
  92.8 0.0 copy-start.1
  92.8 1.7 %copy.17 = bf16[8,16384]{1,0:T(8,128)(2,1)} copy(bf16[8,16384]{1,0:T(8,128)(2,1)} %get-tuple-element.8) | data formatting | bytes 524288
  94.4 0.0 copy-done.1
  94.4 0.0 copy-start
  94.4 0.6 copy.18
  95.1 0.2 copy-done
  95.2 0.0 copy-start.3
  95.2 0.6 copy.19
  95.8 0.1 copy-done.3
  95.9 0.6 copy.20
  (1 shorter events, 0.0 us)
Async XLA Ops:
  0.6 0.7 copy-start.4
  0.6 0.7 copy-start.5
  1.3 0.7 copy-start.2
  92.8 1.7 %copy-start.1 = (bf16[8,2048]{1,0:T(8,128)(2,1)S(1)}, bf16[8,2048]{1,0:T(8,128)(2,1)}, u32[]{:S(2)}) copy-start(bf16[8,2048]{1,0:T(8,128)(2,1)} %get-tuple-element.9) | copy-start | bytes 98308
  94.4 0.8 copy-start
  95.2 0.7 copy-start.3

commit v6 on v3

--- a/solution.py
+++ b/solution.py
@@ -98,7 +98,10 @@
     b_ref,
     c_ref,
     dt_ref,
-    par_ref,
+    weight_ref,
+    bias_ref,
+    rate_ref,
+    skip_ref,
     gx_ref,
     gb_ref,
     gc_ref,
@@ -115,6 +118,7 @@
     gb_all,
     gc_all,
     gdt_all,
+    par_ref,
     head_send,
     head_recv,
     ext,
@@ -169,6 +173,12 @@
             device_id_type=MESH,
         )
 
+    par_ref[0:CONV, :] = weight_ref[...]
+    par_ref[CONV : CONV + 1, :] = bias_ref[...]
+    par_ref[5:8, :] = jnp.zeros((3, width), F32)
+    par_ref[6:7, 0:heads_dev] = rate_ref[...]
+    par_ref[7:8, 0:heads_dev] = skip_ref[...]
+
     barrier = pltpu.get_barrier_semaphore()
     for by in (1, 2, n_ctx - 2, n_ctx - 1):
         pl.semaphore_signal(
@@ -451,10 +461,6 @@
     width = heads_dev * HEAD_DIM
     length = tok_dev * n_head
 
-    wide = lambda value: jnp.pad(value[None, :], ((0, 0), (0, width - heads_dev)))
-    params = jnp.concatenate(
-        [conv_weight, conv_bias[None, :], conv_bias[None, :], wide(decay_rate), wide(skip)], axis=0
-    )
     whole = pltpu.VMEM((STATE, width), F32)
     small = pltpu.VMEM((8, width), F32)
     held = lambda size, kind: pltpu.VMEM((n_head, tok_dev, size), kind)
@@ -468,7 +474,7 @@
             jax.ShapeDtypeStruct(c_in.shape, BF16),
             jax.ShapeDtypeStruct(dt.shape, F32),
         ),
-        in_specs=[pl.BlockSpec(memory_space=pltpu.VMEM)] * 6,
+        in_specs=[pl.BlockSpec(memory_space=pltpu.VMEM)] * 9,
         out_specs=[pl.BlockSpec(memory_space=pltpu.VMEM)] * 4,
         scratch_shapes=[
             held(width, BF16),
@@ -483,6 +489,7 @@
             held(STATE, F32),
             held(STATE, F32),
             held(LANES, BF16),
+            small,
             pltpu.SemaphoreType.DMA((9,)),
             pltpu.SemaphoreType.DMA((9,)),
             pltpu.VMEM((length + 8, width), F32),
@@ -513,7 +520,17 @@
         compiler_params=pltpu.CompilerParams(
             vmem_limit_bytes=56 * 1024 * 1024, collective_id=0, has_side_effects=True
         ),
-    )(x_in, grad_y, b_in, c_in, dt, params)
+    )(
+        x_in,
+        grad_y,
+        b_in,
+        c_in,
+        dt,
+        conv_weight,
+        conv_bias[None, :],
+        decay_rate[None, :],
+        skip[None, :],
+    )
 
 
 def solution(mesh):

time: 96.1 us -> 94.6 us (0.984)
  local copies, waits for them, and re-layouts: 5.73 us -> 3.76 us
    unnamed x16 -> x10, local copies, waits for them, and re-layouts: 4.43 us -> 3.76 us
where the time goes in v6:
time: 94.6 us; the launch traced here: 94.3 us
  Pallas kernels  89.9 us (95%)
  local copies, waits for them, and re-layouts  3.76 us (4%)
    pallas_call x1, Pallas kernels, shards(): pl.pallas_call(functools.partial(block_kernel, n_ctx, n_head), out_shape=...  89.9 us
    unnamed x10, local copies, waits for them, and re-layouts  3.76 us

profile of v6, /device:TPU:1, one launch (start us, length us, event | category | flops | bytes accessed | tf_op | source)
XLA Modules:
  0.0 94.3 jit_solution(350810891376809729)
XLA Ops:
  0.6 89.9 %shard_map.120 = (bf16[8,16384]{1,0:T(8,128)(2,1)}, bf16[8,2048]{1,0:T(8,128)(2,1)}, bf16[8,2048]{1,0:T(8,128)(2,1)}, f32[8,256]{1,0:T(8,128)}) custom-call(bf16[8,16384]{1,0:T(8,128)(2,1)} %x_ref.1, bf16[8,16384]{1,0:T(8,128)(2,1)} %dy_ref.1, bf16[8,2048]{1,0:T(8,128)(2,1)} %b_ref.1, bf16[8,2048]{1,0:T(8,128)(2,1)} %c_ref.1, bf16[8,256]{1,0:T(8,128)(2,1)} %dt_ref.1, ...), custom_call_target="tpu_custom_call" | custom-call | tf_op jit(solution)/shard_map/pallas_call | solution.py:469
  90.6 0.0 copy-start.1
  90.6 1.7 %copy.17 = bf16[8,16384]{1,0:T(8,128)(2,1)} copy(bf16[8,16384]{1,0:T(8,128)(2,1)} %get-tuple-element.8) | data formatting | bytes 524288
  92.3 0.0 copy-done.1
  92.3 0.0 copy-start
  92.3 0.6 copy.18
  92.9 0.2 copy-done
  93.0 0.0 copy-start.2
  93.0 0.6 copy.19
  93.7 0.1 copy-done.2
  93.7 0.6 copy.20
Async XLA Ops:
  90.6 1.7 %copy-start.1 = (bf16[8,2048]{1,0:T(8,128)(2,1)S(1)}, bf16[8,2048]{1,0:T(8,128)(2,1)}, u32[]{:S(2)}) copy-start(bf16[8,2048]{1,0:T(8,128)(2,1)} %get-tuple-element.9) | copy-start | bytes 98308
  92.3 0.8 copy-start
  93.0 0.7 copy-start.2

commit v7 on v6

--- a/solution.py
+++ b/solution.py
@@ -15,7 +15,7 @@
 F32 = jnp.float32
 BF16 = jnp.bfloat16
 MESH = pl.DeviceIdType.MESH
-CHUNK = 16
+CHUNK = 8
 
 
 def nn(a, b):

time: 94.6 us -> 94.1 us (level)
  no operation moved by 1% of the time
where the time goes in v7:
time: 94.1 us; the launch traced here: 93.8 us
  Pallas kernels  89.4 us (95%)
  local copies, waits for them, and re-layouts  3.76 us (4%)
    pallas_call x1, Pallas kernels, shards(): pl.pallas_call(functools.partial(block_kernel, n_ctx, n_head), out_shape=...  89.4 us
    unnamed x10, local copies, waits for them, and re-layouts  3.76 us

profile of v7, /device:TPU:1, one launch (start us, length us, event | category | flops | bytes accessed | tf_op | source)
XLA Modules:
  0.0 93.8 jit_solution(517095707378296148)
XLA Ops:
  0.6 89.4 %shard_map.120 = (bf16[8,16384]{1,0:T(8,128)(2,1)}, bf16[8,2048]{1,0:T(8,128)(2,1)}, bf16[8,2048]{1,0:T(8,128)(2,1)}, f32[8,256]{1,0:T(8,128)}) custom-call(bf16[8,16384]{1,0:T(8,128)(2,1)} %x_ref.1, bf16[8,16384]{1,0:T(8,128)(2,1)} %dy_ref.1, bf16[8,2048]{1,0:T(8,128)(2,1)} %b_ref.1, bf16[8,2048]{1,0:T(8,128)(2,1)} %c_ref.1, bf16[8,256]{1,0:T(8,128)(2,1)} %dt_ref.1, ...), custom_call_target="tpu_custom_call" | custom-call | tf_op jit(solution)/shard_map/pallas_call | solution.py:469
  90.1 0.0 copy-start.1
  90.1 1.7 %copy.17 = bf16[8,16384]{1,0:T(8,128)(2,1)} copy(bf16[8,16384]{1,0:T(8,128)(2,1)} %get-tuple-element.8) | data formatting | bytes 524288
  91.7 0.0 copy-done.1
  91.7 0.0 copy-start
  91.8 0.6 copy.18
  92.4 0.2 copy-done
  92.5 0.0 copy-start.2
  92.5 0.6 copy.19
  93.1 0.1 copy-done.2
  93.2 0.6 copy.20
Async XLA Ops:
  90.1 1.7 %copy-start.1 = (bf16[8,2048]{1,0:T(8,128)(2,1)S(1)}, bf16[8,2048]{1,0:T(8,128)(2,1)}, u32[]{:S(2)}) copy-start(bf16[8,2048]{1,0:T(8,128)(2,1)} %get-tuple-element.9) | copy-start | bytes 98308
  91.7 0.8 copy-start
  92.5 0.7 copy-start.2
